TPU v7x, 128 devices: a whole 4x4x4 slice. The times are simulated.
128 devices in a mesh: sec: 16 (over y, x), dev: 8 (over z, core).
Axes of the slice: x: 4, y: 4, z: 4, core: 2. Of those that a mesh axis runs over, the one named last changes fastest.
Arguments:
- rhs_interior: bfloat16 [1310720, 256], P(('sec', 'dev')), may hold values from -6 to 6
- rhs_interface: float32 [10240, 256], P(('sec', 'dev')), may hold values from -6 to 6
- inv_blocks: bfloat16 [5120, 256, 256], P(('sec', 'dev')), may hold values from -0.375 to 0.375
- coupling: bfloat16 [5120, 2, 64, 256], P(('sec', 'dev')), may hold values from -0.1875 to 0.1875
- interface_map: int32 [5120, 64], P(('sec', 'dev')), may hold values from 0 to 10239, as said below
- slot_counts: int32 [5120], P(('sec', 'dev')), may hold values from 32 to 64, as said below
- column_order: int32 [256], replicated, may hold values from 0 to 255, each once
- schur_inverse: bfloat16 [10240, 10240], P('dev', 'sec'), may hold values from -0.0625 to 0.0625
Outputs:
- interior_solution: bfloat16 [1310720, 256], P(('sec', 'dev'))
- interface_solution: float32 [10240, 256], P('dev')
Inputs may be any that keep to these rules, and one draw needn't show every extreme that they name: `slot_counts`: every block has at least half of its 64 slots live, and some block has all 64 live. `interface_map`: split the interface rows into 128 equal ranges, range d belonging to the device of flat index d over sec+dev; of the 2560 slots of one device's blocks at most 40 point into any one range, the slots into ranges 2p and 2p + 1 together number exactly 40, and one range receives exactly 40 slots from every device.
All inputs are finite; a program needn't handle non-finite values.
Results may differ from a plain program's by a relative error of at most 0.0056.
Values may be sent and summed in bfloat16 or wider, within the bound.
No kernel may reach another device: no remote copies, remote signals or barrier semaphores. Data moves between devices by JAX's collectives and lax.ppermute only.
A program may use at most 128 MiB of HBM per device.

v0:
```python
import jax
import jax.numpy as jnp
from jax import lax
from jax.sharding import PartitionSpec as P


def copy_for_each(array, axis):
    size = lax.axis_size(axis)
    return lax.all_to_all(
        jnp.broadcast_to(array[None], (size, *array.shape)), axis, 0, 0, tiled=True
    )


def in_order(blocks, dim):
    blocks = jnp.moveaxis(blocks, 0, dim)
    lengths = blocks.shape
    return blocks.reshape(*lengths[:dim], lengths[dim] * lengths[dim + 1], *lengths[dim + 2 :])


def gathered_copies(array, axis, dim):
    blocks = copy_for_each(array, axis)
    return in_order(blocks, dim)


def split_up(array, dim, size):
    lengths = array.shape
    blocks = array.reshape(*lengths[:dim], size, lengths[dim] // size, *lengths[dim + 1 :])
    return jnp.moveaxis(blocks, dim, 0)


def sum_at_owner(array, axis, dim):
    size = lax.axis_size(axis)
    blocks = lax.all_to_all(split_up(array, dim, size), axis, 0, 0, tiled=True)
    return jnp.sum(blocks, axis=0)


def rows_for(lines, size):
    spare = -len(lines) % size
    return jnp.pad(lines, [(0, spare)] + [(0, 0)] * (lines.ndim - 1))


def nested_sum(array, axes):
    lines = array.reshape(-1, array.shape[-1])
    own = sum_at_owner(rows_for(lines, lax.axis_size(axes)), axes, 0)
    whole = gathered_copies(own, axes, 0)
    return whole[: len(lines)].reshape(array.shape)


def shards(
    rhs_interior,
    rhs_interface,
    inv_blocks,
    coupling,
    interface_map,
    slot_counts,
    column_order,
    schur_inverse,
):
    block_count = inv_blocks.shape[0]
    block_size = inv_blocks.shape[1]
    slot_count = coupling.shape[2]
    column_count = rhs_interior.shape[1]
    sec_size = lax.axis_size("sec")
    dev_size = lax.axis_size("dev")
    interface_rows = schur_inverse.shape[0] * dev_size
    piece_rows = interface_rows // (sec_size * dev_size)
    live_mask = jnp.arange(slot_count, dtype=jnp.int32)[None, :] < slot_counts[:, None]
    local_rhs = rhs_interior.reshape(block_count, block_size, column_count)
    solved = jnp.einsum(
        "bij,bjn->bin", inv_blocks, local_rhs, preferred_element_type=jnp.float32
    ).astype(jnp.bfloat16)
    solved = lax.optimization_barrier(solved)
    partials = jnp.einsum(
        "bkr,brn->bkn", coupling[:, 0], solved, preferred_element_type=jnp.float32
    )
    partials = jnp.where(live_mask[:, :, None], partials, 0.0).reshape(
        block_count * slot_count, column_count
    )
    rhs_cols = jnp.take(rhs_interface, column_order, axis=1)
    targets = interface_map.reshape(-1)
    owners = sec_size * dev_size
    capacity = 2 * targets.shape[0] // owners
    owner_of = targets // piece_rows
    owner_table = (owner_of[:, None] == jnp.arange(owners, dtype=jnp.int32)[None, :]).astype(
        jnp.int32
    )
    rank = jnp.sum(jnp.cumsum(owner_table, axis=0) * owner_table, axis=1) - 1
    place = owner_of * capacity + rank
    send_rows = jnp.zeros((owners * capacity, column_count), jnp.float32).at[place].set(partials)
    send_index = jnp.zeros((owners * capacity,), jnp.int32).at[place].set(targets % piece_rows)
    recv_rows, recv_index = (
        lax.all_to_all(send_rows, ("sec", "dev"), split_axis=0, concat_axis=0, tiled=True),
        lax.all_to_all(send_index, ("sec", "dev"), split_axis=0, concat_axis=0, tiled=True),
    )
    selector = (jnp.arange(piece_rows, dtype=jnp.int32)[:, None] == recv_index[None, :]).astype(
        jnp.float32
    )
    arrived = jnp.dot(
        selector, recv_rows, precision=lax.Precision.HIGHEST, preferred_element_type=jnp.float32
    )
    reduced = rhs_cols - arrived
    schur_part = jnp.dot(
        schur_inverse,
        gathered_copies(reduced.astype(jnp.bfloat16), "dev", 0),
        preferred_element_type=jnp.float32,
    )
    interface_solution = nested_sum(schur_part, "sec")
    values = lax.all_gather(interface_solution.astype(jnp.bfloat16), "dev", axis=0, tiled=True)
    picked = jnp.take(values, interface_map.reshape(-1), axis=0).reshape(
        block_count, slot_count, column_count
    )
    picked = jnp.where(live_mask[:, :, None], picked, jnp.zeros((), jnp.bfloat16))
    pushed = jnp.einsum(
        "bkr,bkn->brn", coupling[:, 1], picked, preferred_element_type=jnp.float32
    ).astype(jnp.bfloat16)
    back_term = jnp.einsum("bij,bjn->bin", inv_blocks, pushed, preferred_element_type=jnp.float32)
    interior = (solved.astype(jnp.float32) - back_term).astype(jnp.bfloat16)
    return (interior.reshape(block_count * block_size, column_count), interface_solution)


def solution(mesh):
    placed = (
        P(("sec", "dev"), None),
        P(("sec", "dev"), None),
        P(("sec", "dev"), None, None),
        P(("sec", "dev"), None, None, None),
        P(("sec", "dev"), None),
        P(("sec", "dev")),
        P(),
        P("dev", "sec"),
    )
    return jax.shard_map(
        shards,
        mesh=mesh,
        in_specs=placed,
        out_specs=(P(("sec", "dev"), None), P("dev", None)),
        check_vma=False,
    )
```

profile of v0, /device:TPU:1, one launch (start us, length us, event | category | flops | bytes accessed | tf_op | source)
XLA Modules:
  0.0 259.3 jit_solution(17131693676251823404)
XLA Ops:
  7.2 0.0 copy-start
  7.2 0.9 broadcast_remainder_fusion
  8.0 0.1 div.28
  8.1 0.1 div.27
  8.2 0.8 reshape.211
  9.0 0.8 compare_and_fusion
  9.8 0.1 and.44
  9.9 0.1 copy.22
  10.0 0.5 fusion.10
  10.5 0.1 broadcast_add_fusion
  10.7 0.3 copy.23
  10.9 0.1 ne.60
  11.0 0.1 rem.37
  11.1 1.6 fusion.15
  12.7 0.1 fusion.36
  12.8 9.9 %scatter_custom_fusion = s32[5120]{0:T(1024)S(1)} fusion(s32[2560]{0:T(1024)S(1)} %get-tuple-element.3, s32[2560]{0:T(1024)S(1)} %get-tuple-element.9, s32[]{:T(128)} %constant.38.clone.1), kind=kCustom, calls=%fused_computation.54 | custom fusion | bytes 20484 | tf_op jit(solution)/shard_map/scatter | solution.py:90
  22.8 0.7 all_to_all.23
  23.5 11.5 %all-to-all-start = ((s32[128,40,1]{1,2,0:T(1,128)}), s32[128,40,1]{1,2,0:T(1,128)S(1)}, u32[]{:S(2)}, u32[]{:S(2)}) async-start(s32[128,40,1]{1,2,0:T(1,128)} %bitcast.5), calls=%async_computation | async-start | bytes 131072 | tf_op jit(solution)/shard_map/all_to_all | solution.py:93
  35.0 0.0 copy-start.2
  35.0 5.7 %convolution_convert_fusion = bf16[40,256,256]{2,1,0:T(8,128)(2,1)S(1)} fusion(bf16[40,256,256]{2,1,0:T(8,128)(2,1)} %param.10, bf16[40,256,256]{2,1,0:T(8,128)(2,1)} %bitcast.52), kind=kOutput, calls=%fused_computation.9 | convolution fusion | flops 1344798720 | bytes 15728640 | tf_op jit(solution)/shard_map/bij,bjn->bin/dot_general | solution.py:69
  40.7 0.0 copy-start.1
  40.7 2.7 %convolution_select_fusion = f32[40,256,64]{1,2,0:T(8,128)} fusion(bf16[40,256,256]{2,1,0:T(8,128)(2,1)S(1)} %convolution_convert_fusion, bf16[40,2,64,256]{3,2,1,0:T(8,128)(2,1)S(1)} %copy-done.2, pred[40,64]{1,0:T(8,128)(4,1)S(1)} %get-tuple-element.11), kind=kOutput, calls=%fused_computation.13 | convolution fusion | flops 336199680 | bytes 9180160 | tf_op jit(solution)/shard_map/bkr,brn->bkn/dot_general | solution.py:73
  43.4 0.4 copy-done.1
  43.9 14.2 %scatter_custom_fusion.1 = f32[5120,256]{1,0:T(8,128)} fusion(s32[2560]{0:T(1024)S(1)} %get-tuple-element.3, f32[2560,256]{1,0:T(8,128)} %bitcast.53, f32[]{:T(128)} %constant.65.clone.1), kind=kCustom, calls=%fused_computation.11 | custom fusion | bytes 5243392 | tf_op jit(solution)/shard_map/scatter | solution.py:89
  58.0 0.0 all-to-all-done
  58.0 10.2 %all-to-all-start.1 = ((f32[128,40,256]{2,1,0:T(8,128)}), f32[128,40,256]{2,1,0:T(8,128)}, u32[]{:S(2)}, u32[]{:S(2)}) async-start(f32[128,40,256]{2,1,0:T(8,128)} %bitcast.49), calls=%async_computation.1 | async-start | bytes 10485760 | tf_op jit(solution)/shard_map/all_to_all | solution.py:92
  68.2 0.2 all-gather.2.cloned.1.call-start
  68.4 0.1 copy.20
  68.6 0.7 gather_fusion
  69.3 0.1 copy.21
  69.4 0.5 broadcast.209
  69.9 0.8 reduce.7
  70.7 0.1 eq.45
  70.8 61.2 %all-to-all-done.1 = f32[128,40,256]{2,1,0:T(8,128)} async-done(((f32[128,40,256]{2,1,0:T(8,128)}), f32[128,40,256]{2,1,0:T(8,128)}, u32[]{:S(2)}, u32[]{:S(2)}) %all-to-all-start.1) | async-done | bytes 5242912 | tf_op jit(solution)/shard_map/all_to_all | solution.py:92
  132.0 4.7 %fusion.28 = bf16[80,256]{1,0:T(8,128)(2,1)S(1)} fusion(f32[5120,256]{1,0:T(8,128)} %bitcast.10, s32[5120]{0:T(1024)S(1)} %eq.45, f32[256,80]{0,1:T(8,128)S(1)} %copy.21, pred[256]{0:T(512)(128)(4,1)S(1)} %compare_and_fusion.2), kind=kOutput, calls=%fused_computation.31 | convolution fusion | flops 1258762240 | bytes 5386496 | tf_op jit(solution)/shard_map/dot_general | solution.py:98
  136.7 11.0 %all_to_all.36 = bf16[8,80,256]{2,1,0:T(8,128)(2,1)S(1)} all-to-all(bf16[8,80,256]{2,1,0:T(8,128)(2,1)S(1)} %broadcast_in_dim.83), channel_id=1, replica_groups=mesh['sec'=16,'dev'=8] {'dev'}, dimensions={0} | all-to-all | bytes 655360 | tf_op jit(solution)/shard_map/all_to_all | solution.py:9
  147.7 0.7 convolution_bitcast_fusion
  148.5 1.5 copy.26
  149.9 25.4 %all_to_all.37 = f32[16,80,256]{2,1,0:T(8,128)S(1)} all-to-all(f32[16,80,256]{2,1,0:T(8,128)} %bitcast.51), channel_id=1, replica_groups=mesh['sec'=16,'dev'=8] {'sec'}, dimensions={0} | all-to-all | bytes 2621440 | tf_op jit(solution)/shard_map/all_to_all | solution.py:33
  175.4 0.1 reduce_sum.19
  175.5 0.1 broadcast_in_dim.84
  175.6 21.5 %all_to_all.38 = f32[16,80,256]{2,1,0:T(8,128)S(1)} all-to-all(f32[16,80,256]{2,1,0:T(8,128)S(1)} %broadcast_in_dim.84), channel_id=1, replica_groups=mesh['sec'=16,'dev'=8] {'sec'}, dimensions={0} | all-to-all | bytes 2621440 | tf_op jit(solution)/shard_map/all_to_all | solution.py:9
  197.1 0.9 bitcast_convert_fusion
  198.0 0.0 all-gather.2.cloned.1.call-update
  198.0 34.8 %all-gather.2.cloned.1.call-done = bf16[10240,256]{1,0:T(8,128)(2,1)} async-done(((bf16[1280,256]{1,0:T(8,128)(2,1)}), bf16[10240,256]{1,0:T(8,128)(2,1)}) %all-gather.2.cloned.1.call-update) | async-done | bytes 5242896 | tf_op jit(solution)/shard_map/all_gather | solution.py:108
  232.8 10.0 %gather_fusion.1 = bf16[2560,256]{1,0:T(8,128)(2,1)} fusion(bf16[10240,256]{1,0:T(8,128)(2,1)} %all-gather.2.cloned.1.call-done, s32[3072]{0:T(1024)S(1)} %pad_clamp_fusion), kind=kCustom, calls=%fused_computation.1 | custom fusion | bytes 2631680 | tf_op jit(solution)/shard_map/jit(_take)/gather | solution.py:109
  242.8 8.6 %fusion = bf16[40,256,256]{2,1,0:T(8,128)(2,1)} fusion(bf16[40,256,256]{2,1,0:T(8,128)(2,1)} %copy-done.1, bf16[40,256,256]{2,1,0:T(8,128)(2,1)} %param.10, bf16[40,2,64,256]{3,2,1,0:T(8,128)(2,1)} %param.11, bf16[40,64,256]{2,1,0:T(8,128)(2,1)} %bitcast.54, pred[40,64]{1,0:T(8,128)(4,1)S(1)} %get-tuple-element.6, pred[40,64]{1,0:T(8,128)(4,1)S(1)} %get-tuple-element.11), kind=kOutput, calls=%fused_computation.5 | convolution fusion | flops 1689518080 | bytes 18355200 | tf_op jit(solution)/shard_map/bij,bjn->bin/dot_general | solution.py:116
  251.4 1.1 copy.31
  (16 shorter events, 0.1 us)
Async XLA Ops:
  7.2 140.6 %copy-start = (bf16[1280,640]{1,0:T(8,128)(2,1)S(1)}, bf16[1280,640]{1,0:T(8,128)(2,1)}, u32[]{:S(2)}) copy-start(bf16[1280,640]{1,0:T(8,128)(2,1)} %param.15) | copy-start | bytes 4915204
  23.5 34.5 %all-to-all-start = ((s32[128,40,1]{1,2,0:T(1,128)}), s32[128,40,1]{1,2,0:T(1,128)S(1)}, u32[]{:S(2)}, u32[]{:S(2)}) async-start(s32[128,40,1]{1,2,0:T(1,128)} %bitcast.5), calls=%async_computation | async-start | bytes 131072 | tf_op jit(solution)/shard_map/all_to_all | solution.py:93
  35.0 5.8 %copy-start.2 = (bf16[40,2,64,256]{3,2,1,0:T(8,128)(2,1)S(1)}, bf16[40,2,64,256]{3,2,1,0:T(8,128)(2,1)}, u32[]{:S(2)}) copy-start(bf16[40,2,64,256]{3,2,1,0:T(8,128)(2,1)} %param.11) | copy-start | bytes 7864324
  40.7 3.1 %copy-start.1 = (bf16[40,256,256]{2,1,0:T(8,128)(2,1)}, bf16[40,256,256]{2,1,0:T(8,128)(2,1)S(1)}, u32[]{:S(2)}) copy-start(bf16[40,256,256]{2,1,0:T(8,128)(2,1)S(1)} %convolution_convert_fusion) | copy-start | bytes 15728644
  58.0 10.4 %copy-start.3 = (f32[80,256]{1,0:T(8,128)S(1)}, f32[80,256]{1,0:T(8,128)}, u32[]{:S(2)}) copy-start(f32[80,256]{1,0:T(8,128)} %param.9) | copy-start | bytes 245764
  58.0 10.5 %copy-start.4 = (s32[256]{0:T(256)S(1)}, s32[256]{0:T(256)}, u32[]{:S(2)}) copy-start(s32[256]{0:T(256)} %param.14) | copy-start | bytes 3076
  58.0 74.0 %all-to-all-start.1 = ((f32[128,40,256]{2,1,0:T(8,128)}), f32[128,40,256]{2,1,0:T(8,128)}, u32[]{:S(2)}, u32[]{:S(2)}) async-start(f32[128,40,256]{2,1,0:T(8,128)} %bitcast.49), calls=%async_computation.1 | async-start | bytes 10485760 | tf_op jit(solution)/shard_map/all_to_all | solution.py:92
  68.2 164.6 %all-gather.2.cloned.1.call-start = ((), (), s32[]{:S(2)}) async-start(), calls=%async_computation.5 | async-start | bytes 5898240 | tf_op jit(solution)/shard_map/all_gather | solution.py:108
Sparse Core Ops, SparseCore 0:
  198.1 34.6 all-gather.1
where the time goes:
time: 260 us; the launch traced here: 259 us
  waiting for transfers between devices  96 us (37%)
  blocking collectives  57.9 us (22%)
  local copies, waits for them, and re-layouts  41 us (16%)
  matrix products  22.5 us (9%)
  starting transfers between devices  21.9 us (8%)
  between operations  14.3 us (6%)
  other arithmetic  5.83 us (2%)
    all_to_all x1, waiting for transfers between devices, shards(): lax.all_to_all(send_rows, ('sec', 'dev'), split_axis=0, concat_axis=0, ti...  61.2 us
    all_gather x1, waiting for transfers between devices, shards(): lax.all_gather(interface_solution.astype(jnp.bfloat16), 'dev', axis=0, ti...  34.8 us
    all_to_all x2, blocking collectives, copy_for_each(): lax.all_to_all(jnp.broadcast_to(array[None], (size, *array.shape)), axis,...  32.5 us
    all_to_all x1, blocking collectives, sum_at_owner(): blocks = lax.all_to_all(split_up(array, dim, size), axis, 0, 0, tiled=True)  25.4 us
    scatter x1, local copies, waits for them, and re-layouts, shards(): jnp.zeros((owners * capacity, column_count), jnp.float32).at[place]  14.2 us
    all_to_all x1, starting transfers between devices, shards(): lax.all_to_all(send_index, ('sec', 'dev'), split_axis=0, concat_axis=0, t...  11.5 us
    all_to_all x1, starting transfers between devices, shards(): lax.all_to_all(send_rows, ('sec', 'dev'), split_axis=0, concat_axis=0, ti...  10.2 us
    gather x1, local copies, waits for them, and re-layouts, shards(): jnp.take(values, interface_map.reshape(-1), axis=0)  9.97 us
  transfers between devices with their start and end apart: 3, of which 2 were waited for; matrix products, arithmetic and copies ran while one was open for 10% of the time, Pallas kernels for 0%

commit v1 on v0

v1 whole, which is shorter than its diff:
```python
import jax
import jax.numpy as jnp
from jax import lax
from jax.sharding import Mesh
from jax.sharding import PartitionSpec as P

ALL = ("y", "x", "z", "c")
SEC = ("y", "x")
DEV = ("z", "c")
WIRE = 24


def exchange(blocks, axis):
    return lax.all_to_all(blocks, axis, 0, 0, tiled=True)


def copies(array, axis):
    size = lax.axis_size(axis)
    return exchange(jnp.broadcast_to(array[None], (size, *array.shape)), axis)


def strict_lower(n):
    return (jnp.arange(n)[:, None] > jnp.arange(n)[None, :]).astype(jnp.bfloat16)


def shards(
    rhs_interior,
    rhs_interface,
    inv_blocks,
    coupling,
    interface_map,
    slot_counts,
    column_order,
    schur_inverse,
):
    f32, bf16 = jnp.float32, jnp.bfloat16
    nb, n = inv_blocks.shape[:2]
    k = coupling.shape[2]
    cols = rhs_interior.shape[1]
    owners = lax.axis_size(ALL)
    devs = lax.axis_size(DEV)
    secs = lax.axis_size(SEC)
    pairs = owners // 2
    slots = nb * k
    per_pair = slots // pairs
    half = per_pair // 2
    piece = rhs_interface.shape[0]
    pair_rows = 2 * piece
    band = piece * secs
    live = jnp.arange(k, dtype=jnp.int32)[None, :] < slot_counts[:, None]

    pair = interface_map // pair_rows
    off = interface_map % pair_rows
    table = (pair[:, :, None] == jnp.arange(pairs, dtype=jnp.int32)).astype(bf16)
    within = jnp.einsum("kj,bjp->bkp", strict_lower(k), table, preferred_element_type=f32)
    counts = jnp.sum(table.astype(f32), axis=1)
    base = jnp.dot(strict_lower(nb), counts.astype(bf16), preferred_element_type=f32)
    rank = jnp.sum((within + base[:, None, :]) * table.astype(f32), axis=-1).astype(jnp.int32)
    place = (pair * per_pair + rank).reshape(-1)
    wire_place = (place // half) * WIRE + place % half

    solved = jnp.einsum(
        "bij,bjn->bin",
        inv_blocks,
        rhs_interior.reshape(nb, n, cols),
        preferred_element_type=f32,
    ).astype(bf16)
    partials = jnp.einsum("bkr,brn->bkn", coupling[:, 0], solved, preferred_element_type=f32)
    partials = jnp.where(live[:, :, None], partials, 0.0).astype(bf16).reshape(slots, cols)

    mover = jnp.arange(owners * WIRE, dtype=jnp.int32)[:, None] == wire_place[None, :]
    rows = jnp.dot(mover.astype(bf16), partials, preferred_element_type=f32).astype(bf16)
    offs = jnp.sum(jnp.where(mover, off.reshape(1, -1), 0), axis=1).astype(bf16)
    offs = offs.reshape(owners, WIRE)
    spare = jnp.arange(WIRE) >= half
    row_index = jnp.where(spare, -1.0, offs).astype(bf16)
    row_index = jnp.pad(row_index, ((0, 0), (0, cols - WIRE)))[:, None, :]
    wanted = offs[:, :half].reshape(devs, 2, band // pair_rows // 2 * per_pair)
    wanted = jnp.pad(wanted, ((0, 0), (0, 0), (0, cols - wanted.shape[2])))
    wanted = jnp.broadcast_to(wanted[None], (secs, *wanted.shape)).reshape(owners, 2, cols)
    rows = rows.reshape(owners, WIRE, cols)
    sent = jnp.concatenate([rows[:, :half], row_index, wanted, rows[:, half + 3 :]], axis=1)
    got = exchange(sent, ALL)

    target = got[:, half, :WIRE].reshape(1, -1)
    selector = jnp.arange(pair_rows, dtype=jnp.int32)[:, None].astype(bf16) == target
    arrived = jnp.dot(
        selector.astype(bf16), got.reshape(-1, cols), preferred_element_type=f32
    ).reshape(2, piece, cols)
    rhs_cols = jnp.take(rhs_interface, column_order, axis=1)
    mine = jnp.arange(2)[:, None, None] == lax.axis_index("c")
    own = jnp.where(mine, rhs_cols[None], 0.0) - arrived
    reduced = own + lax.ppermute(own, "c", [(0, 1), (1, 0)])
    reduced = reduced.reshape(pair_rows, cols).astype(bf16)
    section = copies(reduced, "z").reshape(-1, cols)

    product = jnp.dot(schur_inverse, section, preferred_element_type=f32)
    parts = exchange(product.astype(bf16).reshape(secs, piece, cols), SEC)
    summed = jnp.sum(parts.astype(f32), axis=0).astype(bf16)
    values = copies(summed, SEC).reshape(band, cols)

    s = lax.axis_index(SEC)
    asked = lax.dynamic_slice_in_dim(got, s * devs, devs, axis=0)[
        :, half + 1 : half + 3, : per_pair * (band // pair_rows) // 2
    ].reshape(devs, band // pair_rows, per_pair)
    picker = asked[:, :, :, None] == jnp.arange(pair_rows, dtype=jnp.int32).astype(bf16)
    returned = jnp.einsum(
        "vjkr,jrn->vjkn",
        picker.astype(bf16),
        values.reshape(-1, pair_rows, cols),
        preferred_element_type=f32,
    ).astype(bf16)
    back = exchange(returned.reshape(devs, -1, cols), DEV).reshape(slots, cols)

    unmover = place[:, None] == jnp.arange(slots, dtype=jnp.int32)[None, :]
    picked = jnp.dot(unmover.astype(bf16), back, preferred_element_type=f32).astype(bf16)
    picked = jnp.where(live[:, :, None], picked.reshape(nb, k, cols), jnp.zeros((), bf16))
    pushed = jnp.einsum(
        "bkr,bkn->brn", coupling[:, 1], picked, preferred_element_type=f32
    ).astype(bf16)
    back_term = jnp.einsum("bij,bjn->bin", inv_blocks, pushed, preferred_element_type=f32)
    interior = (solved.astype(f32) - back_term).astype(bf16)
    return interior.reshape(nb * n, cols), values.astype(f32)


def solution(mesh):
    fine = Mesh(mesh.devices.reshape(4, 4, 4, 2), ALL)
    placed = (
        P(ALL, None),
        P(ALL, None),
        P(ALL, None, None),
        P(ALL, None, None, None),
        P(ALL, None),
        P(ALL),
        P(),
        P(DEV, SEC),
    )
    return jax.shard_map(
        shards,
        mesh=fine,
        in_specs=placed,
        out_specs=(P(ALL, None), P(DEV, None)),
        check_vma=False,
    )
```

time: 260 us -> 148 us (0.57)
  waiting for transfers between devices: 96 us -> 51.1 us
  blocking collectives: 57.9 us -> 23.2 us
  local copies, waits for them, and re-layouts: 41 us -> 6.35 us
  between operations: 14.3 us -> 0.94 us
  matrix products: 22.5 us -> 32.5 us
  other arithmetic: 5.83 us -> 9.69 us
    all_gather x1 -> x0, waiting for transfers between devices: 34.8 us -> none  [shards(): lax.all_gather(interface_solution.astype(jnp.bfloat16), 'dev', axis=0, ti...]
    all_to_all x3 -> x2, blocking collectives: 57.9 us -> 23.2 us  [exchange(): return lax.all_to_all(blocks, axis, 0, 0, tiled=True)]
    scatter x2 -> x0, local copies, waits for them, and re-layouts: 24.1 us -> none  [the longest x1 14.2 us: shards(): jnp.zeros((owners * capacity, column_count), jnp.float32).at[place]]
    dot_general x4 -> x9, matrix products: 19.8 us -> 31.3 us  [the longest x1 10.9 us: shards(): jnp.einsum('bij,bjn->bin', inv_blocks, pushed, preferred_element_type=f32)]
    all_to_all x2 -> x3, waiting for transfers between devices: 61.2 us -> 50.1 us  [exchange(): return lax.all_to_all(blocks, axis, 0, 0, tiled=True)]
    gather x1 -> x0, local copies, waits for them, and re-layouts: 9.97 us -> none  [shards(): jnp.take(values, interface_map.reshape(-1), axis=0)]
    all_to_all x2 -> x3, starting transfers between devices: 21.6 us -> 22.2 us  [exchange(): return lax.all_to_all(blocks, axis, 0, 0, tiled=True)]
  transfers between devices with their start and end apart: 3 -> 4, of which waited for: 2 -> 4; matrix products, arithmetic and copies ran while one was open for 10% -> 2% of each run, Pallas kernels for 0% -> 0%
where the time goes in v1:
time: 148 us; the launch traced here: 147 us
  waiting for transfers between devices  51.1 us (35%)
  matrix products  32.5 us (22%)
  starting transfers between devices  23.7 us (16%)
  blocking collectives  23.2 us (16%)
  other arithmetic  9.69 us (7%)
  local copies, waits for them, and re-layouts  6.35 us (4%)
    all_to_all x3, waiting for transfers between devices, exchange(): return lax.all_to_all(blocks, axis, 0, 0, tiled=True)  50.1 us
    all_to_all x2, blocking collectives, exchange(): return lax.all_to_all(blocks, axis, 0, 0, tiled=True)  23.2 us
    all_to_all x3, starting transfers between devices, exchange(): return lax.all_to_all(blocks, axis, 0, 0, tiled=True)  22.2 us
    dot_general x1, matrix products, shards(): jnp.einsum('bij,bjn->bin', inv_blocks, pushed, preferred_element_type=f32)  10.9 us
    dot_general x1, matrix products, shards(): jnp.dot(unmover.astype(bf16), back, preferred_element_type=f32).astype(bf16)  6.26 us
    dot_general x1, matrix products, shards(): jnp.dot(mover.astype(bf16), partials, preferred_element_type=f32)  5.88 us
    dot_general x1, matrix products, shards(): jnp.einsum('bij,bjn->bin', inv_blocks, rhs_interior.reshape(nb, n, cols),...  5.72 us
    reduce_sum x1, other arithmetic, shards(): offs = jnp.sum(jnp.where(mover, off.reshape(1, -1), 0), axis=1).astype(bf16)  3.44 us
  transfers between devices with their start and end apart: 4, of which 4 were waited for; matrix products, arithmetic and copies ran while one was open for 2% of the time, Pallas kernels for 0%

profile of v1, /device:TPU:1, one launch (start us, length us, event | category | flops | bytes accessed | tf_op | source)
XLA Modules:
  0.0 147.5 jit_solution(10042135706684209318)
XLA Ops:
  0.6 0.0 copy-start
  0.7 0.9 add_select_fusion.1
  1.5 0.4 fusion.41
  2.0 0.1 fusion.52
  2.1 0.6 fusion.37
  2.7 0.8 add_select_fusion
  3.4 0.1 eq.94
  3.5 0.1 broadcast_in_dim.128
  3.6 3.4 %select_reduce_fusion = s32[3072]{0:T(1024)S(1)} fusion(s32[2560]{0:T(1024)S(1)} %broadcast_in_dim.128, s32[2560]{0:T(1024)S(1)} %fusion.54), kind=kLoop, calls=%fused_computation.1 | loop fusion | flops 23589888 | bytes 32768 | tf_op jit(solution)/shard_map/reduce_sum | solution.py:73
  7.0 0.1 convert_element_type.110
  7.2 0.1 copy.34
  7.3 0.1 reshape.162
  7.4 0.7 iota_compare_fusion.14
  8.1 5.7 %convolution_convert_fusion = bf16[40,256,256]{2,1,0:T(8,128)(2,1)S(1)} fusion(bf16[40,256,256]{2,1,0:T(8,128)(2,1)} %param.10, bf16[40,256,256]{2,1,0:T(8,128)(2,1)} %bitcast.69), kind=kOutput, calls=%fused_computation.15 | convolution fusion | flops 1344798720 | bytes 15728640 | tf_op jit(solution)/shard_map/bij,bjn->bin/dot_general | solution.py:62
  13.9 1.1 select_convert_fusion
  15.0 1.2 copy-done.1
  16.2 5.9 %fusion.8 = bf16[3072,256]{1,0:T(8,128)(2,1)S(1)} fusion(bf16[2560,256]{1,0:T(8,128)(2,1)S(1)} %bitcast.76, s32[2560]{0:T(1024)S(1)} %fusion.54), kind=kOutput, calls=%fused_computation.13 | convolution fusion | flops 4035182592 | bytes 2893824 | tf_op jit(solution)/shard_map/dot_general | solution.py:72
  22.1 0.1 slice.32
  22.3 0.1 broadcast_in_dim.132
  22.4 2.0 %pad_maximum_fusion = bf16[128,24,256]{2,1,0:T(8,128)(2,1)} fusion(bf16[128,1,256]{2,1,0:T(2,128)(2,1)S(1)} %slice.32, bf16[128,2,256]{2,1,0:T(2,128)(2,1)S(1)} %bitcast.77, bf16[128,1,256]{2,1,0:T(2,128)(2,1)S(1)} %copy.34, bf16[128,20,256]{2,1,0:T(8,128)(2,1)S(1)} %bitcast.73), kind=kLoop, calls=%fused_computation.24 | loop fusion | flops 6291456 | bytes 3145728 | tf_op jit(solution)/shard_map/concatenate | solution.py:82
  24.4 11.5 %all-to-all-start = ((bf16[128,24,256]{2,1,0:T(8,128)(2,1)}), bf16[128,24,256]{2,1,0:T(8,128)(2,1)S(1)}, u32[]{:S(2)}, u32[]{:S(2)}) async-start(bf16[128,24,256]{2,1,0:T(8,128)(2,1)} %pad_maximum_fusion), calls=%async_computation | async-start | bytes 3145728 | tf_op jit(solution)/shard_map/all_to_all | solution.py:14
  35.9 0.1 copy.31
  36.0 0.7 gather_fusion
  36.8 0.1 select_bitcast_fusion
  36.9 0.1 copy.32
  37.0 23.4 %all-to-all-done = bf16[128,24,256]{2,1,0:T(8,128)(2,1)S(1)} async-done(((bf16[128,24,256]{2,1,0:T(8,128)(2,1)}), bf16[128,24,256]{2,1,0:T(8,128)(2,1)S(1)}, u32[]{:S(2)}, u32[]{:S(2)}) %all-to-all-start) | async-done | bytes 1572896 | tf_op jit(solution)/shard_map/all_to_all | solution.py:14
  60.4 0.2 slice_reduce_fusion
  60.7 0.1 eq.104
  60.8 0.5 fusion.38
  61.2 1.4 collective-permute-start
  62.7 1.0 collective-permute-done
  63.8 9.2 %all_to_all.25 = bf16[4,160,256]{2,1,0:T(8,128)(2,1)S(1)} all-to-all(bf16[4,160,256]{2,1,0:T(8,128)(2,1)S(1)} %broadcast_in_dim.133), channel_id=1, replica_groups=mesh['y'=4,'x'=4,'z'=4,'c'=2] {'z'}, dimensions={0} | all-to-all | bytes 655360 | tf_op jit(solution)/shard_map/all_to_all | solution.py:14
  73.0 0.7 fusion.15
  73.7 0.2 copy.35
  74.0 14.0 %all_to_all.26 = bf16[16,80,256]{2,1,0:T(8,128)(2,1)S(1)} all-to-all(bf16[16,80,256]{2,1,0:T(8,128)(2,1)S(1)} %bitcast.70), channel_id=1, replica_groups=mesh['y'=4,'x'=4,'z'=4,'c'=2] {'y','x'}, dimensions={0} | all-to-all | bytes 1310720 | tf_op jit(solution)/shard_map/all_to_all | solution.py:14
  88.0 0.1 reduce_sum.45
  88.1 0.9 broadcast_in_dim.134
  89.0 3.6 %all-to-all-start.3 = ((bf16[16,80,256]{2,1,0:T(8,128)(2,1)}), bf16[16,80,256]{2,1,0:T(8,128)(2,1)S(1)}, u32[]{:S(2)}, u32[]{:S(2)}) async-start(bf16[16,80,256]{2,1,0:T(8,128)(2,1)} %broadcast_in_dim.134), calls=%async_computation.3 | async-start | bytes 1310720 | tf_op jit(solution)/shard_map/all_to_all | solution.py:14
  92.6 0.8 constant_dynamic-slice_fusion
  93.4 0.1 eq.107
  93.5 10.0 %all-to-all-done.3 = bf16[16,80,256]{2,1,0:T(8,128)(2,1)S(1)} async-done(((bf16[16,80,256]{2,1,0:T(8,128)(2,1)}), bf16[16,80,256]{2,1,0:T(8,128)(2,1)S(1)}, u32[]{:S(2)}, u32[]{:S(2)}) %all-to-all-start.3) | async-done | bytes 655392 | tf_op jit(solution)/shard_map/all_to_all | solution.py:14
  103.4 0.6 fusion.23
  104.0 1.2 copy.37
  105.2 7.2 %all-to-all-start.4 = ((bf16[8,320,256]{2,1,0:T(8,128)(2,1)}), bf16[8,320,256]{2,1,0:T(8,128)(2,1)}, u32[]{:S(2)}, u32[]{:S(2)}) async-start(bf16[8,320,256]{2,1,0:T(8,128)(2,1)} %bitcast.20), calls=%async_computation.4 | async-start | bytes 2621440 | tf_op jit(solution)/shard_map/all_to_all | solution.py:14
  112.4 1.2 bitcast_convert_fusion
  113.6 16.7 %all-to-all-done.4 = bf16[8,320,256]{2,1,0:T(8,128)(2,1)} async-done(((bf16[8,320,256]{2,1,0:T(8,128)(2,1)}), bf16[8,320,256]{2,1,0:T(8,128)(2,1)}, u32[]{:S(2)}, u32[]{:S(2)}) %all-to-all-start.4) | async-done | bytes 1310752 | tf_op jit(solution)/shard_map/all_to_all | solution.py:14
  130.3 6.3 %fusion.7 = bf16[2560,256]{1,0:T(8,128)(2,1)S(1)} fusion(bf16[2560,256]{1,0:T(8,128)(2,1)} %bitcast.21, s32[2560]{0:T(1024)S(1)} %eq.94), kind=kOutput, calls=%fused_computation.12 | convolution fusion | flops 3362652160 | bytes 2631680 | tf_op jit(solution)/shard_map/dot_general | solution.py:116
  136.6 10.9 %fusion.4 = bf16[40,256,256]{2,1,0:T(8,128)(2,1)} fusion(bf16[40,256,256]{2,1,0:T(8,128)(2,1)} %copy-done.1, bf16[40,256,256]{2,1,0:T(8,128)(2,1)} %param.10, bf16[40,2,64,256]{3,2,1,0:T(8,128)(2,1)} %param.11, bf16[40,64,256]{2,1,0:T(8,128)(2,1)S(1)} %bitcast.81, pred[40,64]{1,0:T(8,128)(4,1)S(1)} %iota_compare_fusion.14), kind=kOutput, calls=%fused_computation.9 | convolution fusion | flops 1688862720 | bytes 18352640 | tf_op jit(solution)/shard_map/bij,bjn->bin/dot_general | solution.py:121
  (25 shorter events, 0.2 us)
Async XLA Ops:
  0.6 72.3 %copy-start = (bf16[1280,640]{1,0:T(8,128)(2,1)S(1)}, bf16[1280,640]{1,0:T(8,128)(2,1)}, u32[]{:S(2)}) copy-start(bf16[1280,640]{1,0:T(8,128)(2,1)} %param.15) | copy-start | bytes 4915204
  8.1 5.7 %copy-start.3 = (bf16[40,2,64,256]{3,2,1,0:T(8,128)(2,1)S(1)}, bf16[40,2,64,256]{3,2,1,0:T(8,128)(2,1)}, u32[]{:S(2)}) copy-start(bf16[40,2,64,256]{3,2,1,0:T(8,128)(2,1)} %param.11) | copy-start | bytes 7864324
  13.9 2.4 %copy-start.1 = (bf16[40,256,256]{2,1,0:T(8,128)(2,1)}, bf16[40,256,256]{2,1,0:T(8,128)(2,1)S(1)}, u32[]{:S(2)}) copy-start(bf16[40,256,256]{2,1,0:T(8,128)(2,1)S(1)} %convolution_convert_fusion) | copy-start | bytes 15728644
  22.4 13.5 %copy-start.4 = (f32[80,256]{1,0:T(8,128)S(1)}, f32[80,256]{1,0:T(8,128)}, u32[]{:S(2)}) copy-start(f32[80,256]{1,0:T(8,128)} %param.9) | copy-start | bytes 245764
  22.4 13.6 %copy-start.5 = (s32[256]{0:T(256)S(1)}, s32[256]{0:T(256)}, u32[]{:S(2)}) copy-start(s32[256]{0:T(256)} %param.14) | copy-start | bytes 3076
  24.4 36.0 %all-to-all-start = ((bf16[128,24,256]{2,1,0:T(8,128)(2,1)}), bf16[128,24,256]{2,1,0:T(8,128)(2,1)S(1)}, u32[]{:S(2)}, u32[]{:S(2)}) async-start(bf16[128,24,256]{2,1,0:T(8,128)(2,1)} %pad_maximum_fusion), calls=%async_computation | async-start | bytes 3145728 | tf_op jit(solution)/shard_map/all_to_all | solution.py:14
  60.4 12.5 %copy-start.2 = (bf16[128,24,256]{2,1,0:T(8,128)(2,1)}, bf16[128,24,256]{2,1,0:T(8,128)(2,1)S(1)}, u32[]{:S(2)}) copy-start(bf16[128,24,256]{2,1,0:T(8,128)(2,1)S(1)} %all-to-all-done) | copy-start | bytes 4718596
  61.2 2.5 %collective-permute-start = (f32[2,80,256]{2,1,0:T(8,128)S(1)}, f32[2,80,256]{2,1,0:T(8,128)S(1)}, u32[]{:S(2)}, u32[]{:S(2)}) collective-permute-start(f32[2,80,256]{2,1,0:T(8,128)S(1)} %fusion.38), channel_id=1, source_target_pairs={{0,1},{1,0},{2,3},{3,2},{4,5},{5,4},{6,7},{7,6},{8,9},{9,8},{10,11... | collective-permute-start | bytes 491528 | tf_op jit(solution)/shard_map/ppermute | solution.py:93
  89.0 14.5 %all-to-all-start.3 = ((bf16[16,80,256]{2,1,0:T(8,128)(2,1)}), bf16[16,80,256]{2,1,0:T(8,128)(2,1)S(1)}, u32[]{:S(2)}, u32[]{:S(2)}) async-start(bf16[16,80,256]{2,1,0:T(8,128)(2,1)} %broadcast_in_dim.134), calls=%async_computation.3 | async-start | bytes 1310720 | tf_op jit(solution)/shard_map/all_to_all | solution.py:14
  105.2 25.1 %all-to-all-start.4 = ((bf16[8,320,256]{2,1,0:T(8,128)(2,1)}), bf16[8,320,256]{2,1,0:T(8,128)(2,1)}, u32[]{:S(2)}, u32[]{:S(2)}) async-start(bf16[8,320,256]{2,1,0:T(8,128)(2,1)} %bitcast.20), calls=%async_computation.4 | async-start | bytes 2621440 | tf_op jit(solution)/shard_map/all_to_all | solution.py:14

commit v2 on v1

v2 whole, which is shorter than its diff:
```python
import functools

import jax
import jax.numpy as jnp
from jax import lax
from jax.experimental import pallas as pl
from jax.experimental.pallas import tpu as pltpu
from jax.sharding import Mesh
from jax.sharding import PartitionSpec as P

ALL = ("y", "x", "z", "c")
SEC = ("y", "x")
DEV = ("z", "c")
WIRE = 24
DEAD = 16384
GROUP = 4
F32, BF16 = jnp.float32, jnp.bfloat16


def exchange(blocks, axis):
    return lax.all_to_all(blocks, axis, 0, 0, tiled=True)


def copies(array, axis):
    size = lax.axis_size(axis)
    return exchange(jnp.broadcast_to(array[None], (size, *array.shape)), axis)


def iota(shape, dim):
    return lax.broadcasted_iota(jnp.int32, shape, dim).astype(F32)


def quotient(x, n):
    return jnp.floor((x + 0.5) * (1.0 / n))


def dot(a, b, dims=((1,), (0,))):
    return lax.dot_general(a, b, (dims, ((), ())), preferred_element_type=F32)


def onehot(mask):
    return jnp.where(mask, 1.0, 0.0).astype(BF16)


def forward_kernel(
    sizes, map_ref, rhs_ref, inv_ref, couple_ref, out_ref, place_ref, base_ref, offs_ref
):
    per_pair, half, pair_rows, pairs, devs = sizes
    step = pl.program_id(0)
    n = inv_ref.shape[1]
    k = couple_ref.shape[1]
    lanes = GROUP * k
    tile = 256
    tiles = out_ref.shape[0] // tile

    @pl.when(step == 0)
    def _():
        base_ref[...] = jnp.zeros_like(base_ref)
        offs_ref[...] = jnp.zeros_like(offs_ref)
        out_ref[...] = jnp.zeros_like(out_ref)

    slot = map_ref[0].astype(F32)
    dead = slot >= DEAD
    slot = jnp.where(dead, slot - DEAD, slot)
    pair = quotient(slot, pair_rows)
    off = slot - pair_rows * pair
    table = jnp.where(iota((pairs, lanes), 0) == pair, 1.0, 0.0)
    before = dot(
        table.astype(BF16), onehot(iota((lanes, lanes), 0) < iota((lanes, lanes), 1))
    )
    rank = jnp.sum(table * (before + base_ref[:, :1]), axis=0, keepdims=True)
    base_ref[...] += jnp.sum(table, axis=1, keepdims=True)
    place = pair * per_pair + rank
    place_ref[0] = jnp.where(dead, -1.0, place)
    wire = jnp.where(dead, -1.0, place + (WIRE - half) * quotient(place, half))
    row64 = lax.broadcasted_iota(jnp.int32, (256, lanes), 0) & 63
    offs_ref[...] += dot(
        (table * off).astype(BF16), onehot(row64.astype(F32) == rank), ((1,), (1,))
    )

    parts = []
    for b in range(GROUP):
        solved = dot(inv_ref[b], rhs_ref[b * n : (b + 1) * n, :]).astype(BF16)
        parts.append(dot(couple_ref[b], solved).astype(BF16))
    partials = jnp.concatenate(parts, axis=0)
    for t in range(tiles):
        mover = onehot(iota((tile, lanes), 0) == wire - float(tile * t))
        rows = slice(tile * t, tile * (t + 1))
        out_ref[rows, :] = out_ref[rows, :] + dot(mover, partials).astype(BF16)

    @pl.when(step == pl.num_programs(0) - 1)
    def _():
        offs = offs_ref[...]
        p = lax.broadcasted_iota(jnp.int32, offs.shape, 0)
        lane = lax.broadcasted_iota(jnp.int32, offs.shape, 1)
        spread = jnp.where((lane >> 6) == (p & 3), offs, 0.0).astype(BF16)
        groups = pairs // 4
        wanted = dot(
            onehot(iota((groups, pairs), 0) == quotient(iota((groups, pairs), 1), 4)), spread
        )
        rest = 128 - pairs - groups
        index = jnp.concatenate(
            [offs, wanted, jnp.zeros((rest, offs.shape[1]), F32)], axis=0
        ).astype(BF16)
        for t in range(tiles):
            w = iota((tile, 128), 0) + float(tile * t)
            d = quotient(w, WIRE)
            r = w - WIRE * d
            v = d - devs * quotient(d, devs)
            chosen = jnp.where(
                r == half,
                quotient(d, 2),
                jnp.where(
                    r == half + 1,
                    pairs + 2 * v,
                    jnp.where(r == half + 2, pairs + 1 + 2 * v, -1.0),
                ),
            )
            rows = slice(tile * t, tile * (t + 1))
            picker = onehot(iota((tile, 128), 1) == chosen)
            out_ref[rows, :] = out_ref[rows, :] + dot(picker, index).astype(BF16)


def middle_kernel(rhs_ref, inv_ref, couple_ref, solved_ref, w_ref):
    n = inv_ref.shape[1]
    for b in range(inv_ref.shape[0]):
        rows = slice(b * n, (b + 1) * n)
        solved_ref[rows, :] = dot(inv_ref[b], rhs_ref[rows, :]).astype(BF16)
        w_ref[b] = dot(inv_ref[b], couple_ref[b], ((1,), (1,))).astype(BF16)


def tail_kernel(place_ref, back_ref, solved_ref, w_ref, out_ref):
    n = w_ref.shape[1]
    k = w_ref.shape[2]
    slots = back_ref.shape[0]
    lanes = place_ref.shape[0]
    mover = onehot(place_ref[...] == iota((lanes, slots), 1))
    picked = dot(mover, back_ref[...]).astype(BF16)
    for b in range(w_ref.shape[0]):
        rows = slice(b * n, (b + 1) * n)
        term = dot(w_ref[b], picked[b * k : (b + 1) * k, :])
        out_ref[rows, :] = (solved_ref[rows, :].astype(F32) - term).astype(BF16)


def cost(flops, size):
    return pl.CostEstimate(flops=flops, bytes_accessed=size, transcendentals=0)


def shards(
    rhs_interior,
    rhs_interface,
    inv_blocks,
    coupling,
    interface_map,
    slot_counts,
    column_order,
    schur_inverse,
):
    f32, bf16 = F32, BF16
    nb, n = inv_blocks.shape[:2]
    k = coupling.shape[2]
    cols = rhs_interior.shape[1]
    owners = lax.axis_size(ALL)
    devs = lax.axis_size(DEV)
    secs = lax.axis_size(SEC)
    pairs = owners // 2
    slots = nb * k
    per_pair = slots // pairs
    half = per_pair // 2
    piece = rhs_interface.shape[0]
    pair_rows = 2 * piece
    band = piece * secs
    steps = nb // GROUP
    lanes = GROUP * k

    live = jnp.arange(k, dtype=jnp.int32)[None, :] < slot_counts[:, None]
    marked = jnp.where(live, interface_map, interface_map + DEAD).reshape(steps, 1, lanes)
    block_specs = [
        pl.BlockSpec((GROUP * n, cols), lambda i: (i, 0)),
        pl.BlockSpec((GROUP, n, n), lambda i: (i, 0, 0)),
    ]
    sent, place = pl.pallas_call(
        functools.partial(forward_kernel, (per_pair, half, pair_rows, pairs, devs)),
        grid=(steps,),
        in_specs=[
            pl.BlockSpec((1, 1, lanes), lambda i: (i, 0, 0)),
            *block_specs,
            pl.BlockSpec((GROUP, None, k, n), lambda i: (i, 0, 0, 0)),
        ],
        out_specs=[
            pl.BlockSpec((owners * WIRE, cols), lambda i: (0, 0)),
            pl.BlockSpec((1, 1, lanes), lambda i: (i, 0, 0)),
        ],
        out_shape=[
            jax.ShapeDtypeStruct((owners * WIRE, cols), bf16),
            jax.ShapeDtypeStruct((steps, 1, lanes), f32),
        ],
        scratch_shapes=[pltpu.VMEM((pairs, 128), f32), pltpu.VMEM((pairs, 256), f32)],
        cost_estimate=cost(6 * 10**9, 14 * 10**6),
        name="forward",
    )(marked, rhs_interior, inv_blocks, coupling)
    got = exchange(sent.reshape(owners, WIRE, cols), ALL)
    solved, weights = pl.pallas_call(
        middle_kernel,
        grid=(steps,),
        in_specs=[*block_specs, pl.BlockSpec((GROUP, None, k, n), lambda i: (i, 1, 0, 0))],
        out_specs=[
            pl.BlockSpec((GROUP * n, cols), lambda i: (i, 0)),
            pl.BlockSpec((GROUP, n, k), lambda i: (i, 0, 0)),
        ],
        out_shape=[
            jax.ShapeDtypeStruct((nb * n, cols), bf16),
            jax.ShapeDtypeStruct((nb, n, k), bf16),
        ],
        cost_estimate=cost(2 * 10**9, 20 * 10**6),
        name="middle",
    )(rhs_interior, inv_blocks, coupling)

    core = lax.axis_index("c")
    offs = jnp.where(core == 0, got[:, half, :half], got[:, half, half : 2 * half])
    target = jnp.pad(offs, ((0, 0), (0, WIRE - half)), constant_values=-1.0).reshape(1, -1)
    selector = jnp.arange(pair_rows, dtype=jnp.int32)[:, None].astype(bf16) == target
    arrived = jnp.dot(
        selector.astype(bf16), got.reshape(-1, cols), preferred_element_type=f32
    ).reshape(2, piece, cols)
    rhs_cols = jnp.take(rhs_interface, column_order, axis=1)
    mine = jnp.arange(2)[:, None, None] == core
    own = jnp.where(mine, rhs_cols[None], 0.0) - arrived
    reduced = own + lax.ppermute(own, "c", [(0, 1), (1, 0)])
    reduced = reduced.reshape(pair_rows, cols).astype(bf16)
    section = copies(reduced, "z").reshape(-1, cols)

    product = jnp.dot(schur_inverse, section, preferred_element_type=f32)
    parts = exchange(product.astype(bf16).reshape(secs, piece, cols), SEC)
    summed = jnp.sum(parts.astype(f32), axis=0).astype(bf16)
    values = copies(summed, SEC).reshape(band, cols)

    s = lax.axis_index(SEC)
    asked = lax.dynamic_slice_in_dim(got[:, half + 1 : half + 3], s * devs, devs, axis=0)
    asked = asked.reshape(devs, band // pair_rows, 64)[:, :, :per_pair]
    picker = asked[:, :, :, None] == jnp.arange(pair_rows, dtype=jnp.int32).astype(bf16)
    returned = jnp.einsum(
        "vjkr,jrn->vjkn",
        picker.astype(bf16),
        values.reshape(-1, pair_rows, cols),
        preferred_element_type=f32,
    ).astype(bf16)
    back = exchange(returned.reshape(devs, -1, cols), DEV).reshape(slots, cols)

    interior = pl.pallas_call(
        tail_kernel,
        grid=(steps,),
        in_specs=[
            pl.BlockSpec((lanes, 1), lambda i: (i, 0)),
            pl.BlockSpec((slots, cols), lambda i: (0, 0)),
            pl.BlockSpec((GROUP * n, cols), lambda i: (i, 0)),
            pl.BlockSpec((GROUP, n, k), lambda i: (i, 0, 0)),
        ],
        out_specs=pl.BlockSpec((GROUP * n, cols), lambda i: (i, 0)),
        out_shape=jax.ShapeDtypeStruct((nb * n, cols), bf16),
        cost_estimate=cost(4 * 10**9, 14 * 10**6),
        name="tail",
    )(place.reshape(slots, 1), back, solved, weights)
    return interior, values.astype(f32)


def solution(mesh):
    fine = Mesh(mesh.devices.reshape(4, 4, 4, 2), ALL)
    placed = (
        P(ALL, None),
        P(ALL, None),
        P(ALL, None, None),
        P(ALL, None, None, None),
        P(ALL, None),
        P(ALL),
        P(),
        P(DEV, SEC),
    )
    return jax.shard_map(
        shards,
        mesh=fine,
        in_specs=placed,
        out_specs=(P(ALL, None), P(DEV, None)),
        check_vma=False,
    )
```

time: 148 us -> 143 us (0.966)
  Pallas kernels: 0 us -> 45.2 us
  matrix products: 32.5 us -> 1.82 us
  waiting for transfers between devices: 51.1 us -> 36.1 us
  other arithmetic: 9.69 us -> 3.43 us
  local copies, waits for them, and re-layouts: 6.35 us -> 8.46 us
    pallas_call x0 -> x3, Pallas kernels: none -> 45.2 us  [the longest x1 19 us: shards(): pl.pallas_call(functools.partial(forward_kernel, (per_pair, half, pair_ro...]
    dot_general x7 -> x0, matrix products: 30.6 us -> none  [the longest x1 10.9 us: shards(): jnp.einsum('bij,bjn->bin', inv_blocks, pushed, preferred_element_type=f32)]
    all_to_all x3, waiting for transfers between devices: 50.1 us -> 35.1 us  [exchange(): return lax.all_to_all(blocks, axis, 0, 0, tiled=True)]
    reduce_sum x2 -> x0, other arithmetic: 3.86 us -> none  [the longest x1 3.44 us: shards(): offs = jnp.sum(jnp.where(mover, off.reshape(1, -1), 0), axis=1).astype(bf16)]
    reshape x1 -> x3, local copies, waits for them, and re-layouts: 0.11 us -> 2.38 us  [the longest x1 1.6 us: shards(): place.reshape(slots, 1)]
    concatenate x1 -> x0, other arithmetic: 1.98 us -> none  [shards(): jnp.concatenate([rows[:, :half], row_index, wanted, rows[:, half + 3:]],...]
  transfers between devices with their start and end apart: 4 -> 4, of which waited for: 4 -> 4; matrix products, arithmetic and copies ran while one was open for 2% -> 4% of each run, Pallas kernels for 0% -> 8%
where the time goes in v2:
time: 143 us; the launch traced here: 142 us
  Pallas kernels  45.2 us (32%)
  waiting for transfers between devices  36.1 us (25%)
  starting transfers between devices  23.2 us (16%)
  blocking collectives  23.2 us (16%)
  local copies, waits for them, and re-layouts  8.46 us (6%)
  other arithmetic  3.43 us (2%)
  matrix products  1.82 us (1%)
    all_to_all x3, waiting for transfers between devices, exchange(): return lax.all_to_all(blocks, axis, 0, 0, tiled=True)  35.1 us
    all_to_all x2, blocking collectives, exchange(): return lax.all_to_all(blocks, axis, 0, 0, tiled=True)  23.2 us
    all_to_all x3, starting transfers between devices, exchange(): return lax.all_to_all(blocks, axis, 0, 0, tiled=True)  21.7 us
    pallas_call x1, Pallas kernels, shards(): pl.pallas_call(functools.partial(forward_kernel, (per_pair, half, pair_ro...  19 us
    pallas_call x1, Pallas kernels, shards(): pl.pallas_call(tail_kernel, grid=(steps,), in_specs=[pl.BlockSpec((lanes,...  14.3 us
    pallas_call x1, Pallas kernels, shards(): pl.pallas_call(middle_kernel, grid=(steps,), in_specs=[*block_specs, pl.B...  11.8 us
  transfers between devices with their start and end apart: 4, of which 4 were waited for; matrix products, arithmetic and copies ran while one was open for 4% of the time, Pallas kernels for 8%

profile of v2, /device:TPU:1, one launch (start us, length us, event | category | flops | bytes accessed | tf_op | source)
XLA Modules:
  0.0 142.3 jit_solution(397344510023130450)
XLA Ops:
  0.6 0.0 copy-start
  0.6 0.9 add_select_fusion
  1.6 0.7 reshape.99.map_ref
  2.3 19.0 %forward.1 = (bf16[3072,256]{1,0:T(8,128)(2,1)}, f32[10,1,256]{2,1,0:T(1,128)}) custom-call(s32[10,1,256]{2,1,0:T(1,128)} %reshape.99.map_ref, bf16[10240,256]{1,0:T(8,128)(2,1)} %rhs_ref.3, bf16[40,256,256]{2,1,0:T(8,128)(2,1)} %inv_ref.3, bf16[40,2,64,256]{3,2,1,0:T(8,128)(2,1)} %couple_ref.3), custom_call_target="tpu_custom_call" | custom-call | flops 6000000000 | bytes 14000000 | tf_op jit(solution)/shard_map/forward/pallas_call | solution.py:182
  21.3 0.0 copy-start.4
  21.3 0.0 copy-start.6
  21.3 11.5 %all-to-all-start = ((bf16[128,24,256]{2,1,0:T(8,128)(2,1)}), bf16[128,24,256]{2,1,0:T(8,128)(2,1)S(1)}, u32[]{:S(2)}, u32[]{:S(2)}) async-start(bf16[128,24,256]{2,1,0:T(8,128)(2,1)} %bitcast.35), calls=%async_computation | async-start | bytes 3145728 | tf_op jit(solution)/shard_map/all_to_all | solution.py:21
  32.8 0.0 copy-done.4
  32.8 0.1 copy.22
  32.9 0.0 copy-done.6
  33.0 0.7 gather_fusion
  33.7 0.1 select_bitcast_fusion
  33.8 0.1 copy.23
  33.9 23.4 %all-to-all-done = bf16[128,24,256]{2,1,0:T(8,128)(2,1)S(1)} async-done(((bf16[128,24,256]{2,1,0:T(8,128)(2,1)}), bf16[128,24,256]{2,1,0:T(8,128)(2,1)S(1)}, u32[]{:S(2)}, u32[]{:S(2)}) %all-to-all-start) | async-done | bytes 1572896 | tf_op jit(solution)/shard_map/all_to_all | solution.py:21
  57.4 0.0 copy-start.3
  57.4 0.2 fusion.18
  57.5 0.1 copy.32
  57.6 0.1 copy.33
  57.7 0.1 copy.34
  57.9 0.1 eq.51
  58.0 0.5 fusion.11
  58.5 1.4 %collective-permute-start = (f32[2,80,256]{2,1,0:T(8,128)S(1)}, f32[2,80,256]{2,1,0:T(8,128)S(1)}, u32[]{:S(2)}, u32[]{:S(2)}) collective-permute-start(f32[2,80,256]{2,1,0:T(8,128)S(1)} %fusion.11), channel_id=1, source_target_pairs={{0,1},{1,0},{2,3},{3,2},{4,5},{5,4},{6,7},{7,6},{8,9},{9,8},{10,11... | collective-permute-start | bytes 491528 | tf_op jit(solution)/shard_map/ppermute | solution.py:229
  59.9 1.0 collective-permute-done
  61.0 0.0 copy-done.3
  61.0 9.2 %all_to_all.25 = bf16[4,160,256]{2,1,0:T(8,128)(2,1)S(1)} all-to-all(bf16[4,160,256]{2,1,0:T(8,128)(2,1)S(1)} %broadcast_in_dim.57), channel_id=1, replica_groups=mesh['y'=4,'x'=4,'z'=4,'c'=2] {'z'}, dimensions={0} | all-to-all | bytes 655360 | tf_op jit(solution)/shard_map/all_to_all | solution.py:21
  70.2 0.0 copy-done
  70.2 0.7 fusion.2
  70.9 0.2 copy.27
  71.2 14.0 %all_to_all.26 = bf16[16,80,256]{2,1,0:T(8,128)(2,1)S(1)} all-to-all(bf16[16,80,256]{2,1,0:T(8,128)(2,1)S(1)} %bitcast.32), channel_id=1, replica_groups=mesh['y'=4,'x'=4,'z'=4,'c'=2] {'y','x'}, dimensions={0} | all-to-all | bytes 1310720 | tf_op jit(solution)/shard_map/all_to_all | solution.py:21
  85.2 0.1 reduce_sum.12
  85.3 0.9 broadcast_in_dim.58
  86.2 3.6 %all-to-all-start.3 = ((bf16[16,80,256]{2,1,0:T(8,128)(2,1)}), bf16[16,80,256]{2,1,0:T(8,128)(2,1)S(1)}, u32[]{:S(2)}, u32[]{:S(2)}) async-start(bf16[16,80,256]{2,1,0:T(8,128)(2,1)} %broadcast_in_dim.58), calls=%async_computation.3 | async-start | bytes 1310720 | tf_op jit(solution)/shard_map/all_to_all | solution.py:21
  89.8 1.2 slice.20
  91.0 0.1 reshape.105
  91.1 9.5 %all-to-all-done.3 = bf16[16,80,256]{2,1,0:T(8,128)(2,1)S(1)} async-done(((bf16[16,80,256]{2,1,0:T(8,128)(2,1)}), bf16[16,80,256]{2,1,0:T(8,128)(2,1)S(1)}, u32[]{:S(2)}, u32[]{:S(2)}) %all-to-all-start.3) | async-done | bytes 655392 | tf_op jit(solution)/shard_map/all_to_all | solution.py:21
  100.6 0.0 copy-start.2
  100.6 0.6 fusion.8
  101.3 1.1 copy.29
  102.4 0.0 copy-done.2
  102.4 0.0 copy-start.5
  102.4 6.6 %all-to-all-start.4 = ((bf16[8,320,256]{2,1,0:T(8,128)(2,1)}), bf16[8,320,256]{2,1,0:T(8,128)(2,1)S(1)}, u32[]{:S(2)}, u32[]{:S(2)}) async-start(bf16[8,320,256]{2,1,0:T(8,128)(2,1)} %bitcast.14), calls=%async_computation.4 | async-start | bytes 2621440 | tf_op jit(solution)/shard_map/all_to_all | solution.py:21
  109.1 0.0 copy-done.5
  109.1 1.6 %copy.30.place_ref = f32[2560,1]{1,0:T(8,128)} copy(f32[2560,1]{0,1:T(1,128)S(1)} %bitcast.39) | data formatting | bytes 20480 | tf_op jit(solution)/shard_map/reshape | solution.py:263
  110.7 11.8 %middle.1 = (bf16[10240,256]{1,0:T(8,128)(2,1)}, bf16[40,256,64]{2,1,0:T(8,128)(2,1)}) custom-call(bf16[10240,256]{1,0:T(8,128)(2,1)} %rhs_ref.3, bf16[40,256,256]{2,1,0:T(8,128)(2,1)} %inv_ref.3, bf16[40,2,64,256]{3,2,1,0:T(8,128)(2,1)} %couple_ref.3), custom_call_target="tpu_custom_call" | custom-call | flops 2000000000 | bytes 20000000 | tf_op jit(solution)/shard_map/middle/pallas_call | solution.py:203
  122.5 2.2 %bitcast_convert_fusion = f32[1280,256]{1,0:T(8,128)} fusion(bf16[16,80,256]{2,1,0:T(8,128)(2,1)} %copy-done.2), kind=kLoop, calls=%fused_computation.10 | loop fusion | flops 327680 | bytes 1966080 | tf_op jit(solution)/shard_map/convert_element_type | solution.py:264
  124.7 2.1 %all-to-all-done.4 = bf16[8,320,256]{2,1,0:T(8,128)(2,1)S(1)} async-done(((bf16[8,320,256]{2,1,0:T(8,128)(2,1)}), bf16[8,320,256]{2,1,0:T(8,128)(2,1)S(1)}, u32[]{:S(2)}, u32[]{:S(2)}) %all-to-all-start.4) | async-done | bytes 1310752 | tf_op jit(solution)/shard_map/all_to_all | solution.py:21
  126.9 1.1 copy-done.1
  127.9 14.3 %tail.1 = bf16[10240,256]{1,0:T(8,128)(2,1)} custom-call(f32[2560,1]{1,0:T(8,128)} %copy.30.place_ref, bf16[2560,256]{1,0:T(8,128)(2,1)} %bitcast.31, bf16[10240,256]{1,0:T(8,128)(2,1)} %get-tuple-element.8.solved_ref, bf16[40,256,64]{2,1,0:T(8,128)(2,1)} %get-tuple-element.9.w_ref), custom_call_target="tpu_custom_call" | custom-call | flops 4000000000 | bytes 14000000 | tf_op jit(solution)/shard_map/tail/pallas_call | solution.py:250
  (13 shorter events, 0.1 us)
Async XLA Ops:
  0.6 69.6 %copy-start = (bf16[1280,640]{1,0:T(8,128)(2,1)S(1)}, bf16[1280,640]{1,0:T(8,128)(2,1)}, u32[]{:S(2)}) copy-start(bf16[1280,640]{1,0:T(8,128)(2,1)} %param.15) | copy-start | bytes 4915204
  21.3 11.5 %copy-start.4 = (f32[80,256]{1,0:T(8,128)S(1)}, f32[80,256]{1,0:T(8,128)}, u32[]{:S(2)}) copy-start(f32[80,256]{1,0:T(8,128)} %param.9) | copy-start | bytes 245764
  21.3 11.6 %copy-start.6 = (s32[256]{0:T(256)S(1)}, s32[256]{0:T(256)}, u32[]{:S(2)}) copy-start(s32[256]{0:T(256)} %param.14) | copy-start | bytes 3076
  21.3 36.0 %all-to-all-start = ((bf16[128,24,256]{2,1,0:T(8,128)(2,1)}), bf16[128,24,256]{2,1,0:T(8,128)(2,1)S(1)}, u32[]{:S(2)}, u32[]{:S(2)}) async-start(bf16[128,24,256]{2,1,0:T(8,128)(2,1)} %bitcast.35), calls=%async_computation | async-start | bytes 3145728 | tf_op jit(solution)/shard_map/all_to_all | solution.py:21
  57.4 3.6 %copy-start.3 = (bf16[128,24,256]{2,1,0:T(8,128)(2,1)}, bf16[128,24,256]{2,1,0:T(8,128)(2,1)S(1)}, u32[]{:S(2)}) copy-start(bf16[128,24,256]{2,1,0:T(8,128)(2,1)S(1)} %all-to-all-done) | copy-start | bytes 4718596
  58.5 2.5 %collective-permute-start = (f32[2,80,256]{2,1,0:T(8,128)S(1)}, f32[2,80,256]{2,1,0:T(8,128)S(1)}, u32[]{:S(2)}, u32[]{:S(2)}) collective-permute-start(f32[2,80,256]{2,1,0:T(8,128)S(1)} %fusion.11), channel_id=1, source_target_pairs={{0,1},{1,0},{2,3},{3,2},{4,5},{5,4},{6,7},{7,6},{8,9},{9,8},{10,11... | collective-permute-start | bytes 491528 | tf_op jit(solution)/shard_map/ppermute | solution.py:229
  86.2 14.5 %all-to-all-start.3 = ((bf16[16,80,256]{2,1,0:T(8,128)(2,1)}), bf16[16,80,256]{2,1,0:T(8,128)(2,1)S(1)}, u32[]{:S(2)}, u32[]{:S(2)}) async-start(bf16[16,80,256]{2,1,0:T(8,128)(2,1)} %broadcast_in_dim.58), calls=%async_computation.3 | async-start | bytes 1310720 | tf_op jit(solution)/shard_map/all_to_all | solution.py:21
  100.6 1.8 %copy-start.2 = (bf16[16,80,256]{2,1,0:T(8,128)(2,1)}, bf16[16,80,256]{2,1,0:T(8,128)(2,1)S(1)}, u32[]{:S(2)}) copy-start(bf16[16,80,256]{2,1,0:T(8,128)(2,1)S(1)} %all-to-all-done.3) | copy-start | bytes 1966084
  102.4 6.6 %copy-start.5 = (f32[10,1,256]{2,1,0:T(1,128)S(1)}, f32[10,1,256]{2,1,0:T(1,128)}, u32[]{:S(2)}) copy-start(f32[10,1,256]{2,1,0:T(1,128)} %get-tuple-element.6) | copy-start | bytes 30724
  102.4 24.5 %all-to-all-start.4 = ((bf16[8,320,256]{2,1,0:T(8,128)(2,1)}), bf16[8,320,256]{2,1,0:T(8,128)(2,1)S(1)}, u32[]{:S(2)}, u32[]{:S(2)}) async-start(bf16[8,320,256]{2,1,0:T(8,128)(2,1)} %bitcast.14), calls=%async_computation.4 | async-start | bytes 2621440 | tf_op jit(solution)/shard_map/all_to_all | solution.py:21
  126.9 1.1 copy-start.1

commit v3 on v2

v3 whole, which is shorter than its diff:
```python
import functools

import jax
import jax.numpy as jnp
from jax import lax
from jax.experimental import pallas as pl
from jax.experimental.pallas import tpu as pltpu
from jax.sharding import Mesh
from jax.sharding import PartitionSpec as P

ALL = ("y", "x", "z", "c")
SEC = ("y", "x")
DEV = ("z", "c")
WIRE = 24
GROUP = 4
F32, BF16 = jnp.float32, jnp.bfloat16


def exchange(blocks, axis):
    return lax.all_to_all(blocks, axis, 0, 0, tiled=True)


def copies(array, axis):
    size = lax.axis_size(axis)
    return exchange(jnp.broadcast_to(array[None], (size, *array.shape)), axis)


def iota(shape, dim):
    return lax.broadcasted_iota(jnp.int32, shape, dim).astype(F32)


def quotient(x, n):
    return jnp.floor((x + 0.5) * (1.0 / n))


def dot(a, b, dims=((1,), (0,))):
    return lax.dot_general(a, b, (dims, ((), ())), preferred_element_type=F32)


def onehot(mask):
    return jnp.where(mask, 1.0, 0.0).astype(BF16)


def rank_kernel(sizes, counts_ref, map_ref, wire_ref, place_ref, index_ref):
    per_pair, half, pair_rows, pairs, owners = sizes
    blocks, k = map_ref.shape
    lanes = GROUP * k
    upper = onehot(iota((lanes, lanes), 0) < iota((lanes, lanes), 1))
    row64 = (lax.broadcasted_iota(jnp.int32, (256, lanes), 0) & 63).astype(F32)
    lane = lax.broadcasted_iota(jnp.int32, (1, k), 1)
    wire_ref[0:1, :] = jnp.full((1, lanes), owners * WIRE, jnp.int32)
    place_ref[blocks // GROUP :, :] = jnp.full((1, lanes), pairs * per_pair, jnp.int32)
    base = jnp.zeros((pairs, 1), F32)
    offs = jnp.zeros((pairs, 256), F32)
    for g in range(blocks // GROUP):
        mine = range(g * GROUP, (g + 1) * GROUP)
        slot = jnp.concatenate([map_ref[b : b + 1, :] for b in mine], axis=1).astype(F32)
        live = jnp.concatenate(
            [jnp.where(lane < counts_ref[b], 1.0, 0.0) for b in mine], axis=1
        )
        dead = live == 0.0
        pair = quotient(slot, pair_rows)
        off = slot - pair_rows * pair
        table = jnp.where(iota((pairs, lanes), 0) == pair, 1.0, 0.0)
        before = dot(table.astype(BF16), upper)
        rank = jnp.sum(table * (before + base), axis=0, keepdims=True)
        base = base + jnp.sum(table, axis=1, keepdims=True)
        place = pair * per_pair + rank
        wire = place + (WIRE - half) * quotient(place, half)
        place_ref[g : g + 1, :] = jnp.where(dead, pairs * per_pair, place).astype(jnp.int32)
        wire_ref[g + 1 : g + 2, :] = jnp.where(dead, owners * WIRE, wire).astype(jnp.int32)
        offs = offs + dot((table * off).astype(BF16), onehot(row64 == rank), ((1,), (1,)))
    p = lax.broadcasted_iota(jnp.int32, offs.shape, 0)
    at = lax.broadcasted_iota(jnp.int32, offs.shape, 1)
    spread = jnp.where((at >> 6) == (p & 3), offs, 0.0).astype(BF16)
    groups = pairs // 4
    member = iota((groups, pairs), 0) == quotient(iota((groups, pairs), 1), 4)
    index_ref[:pairs, :] = offs
    index_ref[pairs:, :] = dot(onehot(member), spread)


def forward_kernel(
    sizes, wire_ref, index_ref, rhs_ref, inv_ref, couple_ref, out_ref, wide_ref, stage_ref
):
    half, pairs, devs = sizes
    step = pl.program_id(0)
    n = inv_ref.shape[1]
    k = couple_ref.shape[1]
    lanes = GROUP * k
    rows_out = out_ref.shape[0]

    @pl.when(step == 0)
    def _():
        wide_ref[...] = jnp.zeros_like(wide_ref)
        stage_ref[...] = jnp.zeros_like(stage_ref)
        for d in range(rows_out // WIRE):
            v = d % devs
            for r, m in enumerate((d // 2, pairs + 2 * v, pairs + 2 * v + 1)):
                w = d * WIRE + half + r
                wide_ref[0, w : w + 1, :] = index_ref[m : m + 1, :128]
                wide_ref[1, w : w + 1, :] = index_ref[m : m + 1, 128:]

    def move(step, first, last):
        here = wire_ref.at[pl.ds(step * lanes, lanes)]
        for i in range(first, last):
            row = pl.ds(here[i], 1)
            wide_ref[:, row, :] = stage_ref[:, i : i + 1, :]

    solved = [
        dot(inv_ref[b], rhs_ref[b * n : (b + 1) * n, :]).astype(BF16) for b in range(GROUP)
    ]
    move(step, 0, lanes // 2)
    parts = [dot(couple_ref[b], solved[b]) for b in range(GROUP)]
    move(step, lanes // 2, lanes)
    for b in range(GROUP):
        own = slice(b * k, (b + 1) * k)
        stage_ref[0, own, :] = parts[b][:, :128]
        stage_ref[1, own, :] = parts[b][:, 128:]

    @pl.when(step == pl.num_programs(0) - 1)
    def _():
        move(step + 1, 0, lanes)
        for t in range(rows_out // 256):
            rows = slice(256 * t, 256 * (t + 1))
            out_ref[rows, :128] = wide_ref[0, rows, :].astype(BF16)
            out_ref[rows, 128:] = wide_ref[1, rows, :].astype(BF16)


def middle_kernel(rhs_ref, inv_ref, couple_ref, solved_ref, w_ref):
    n = inv_ref.shape[1]
    for b in range(inv_ref.shape[0]):
        rows = slice(b * n, (b + 1) * n)
        solved_ref[rows, :] = dot(inv_ref[b], rhs_ref[rows, :]).astype(BF16)
        w_ref[b] = dot(inv_ref[b], couple_ref[b], ((1,), (1,))).astype(BF16)


def tail_kernel(place_ref, back_ref, solved_ref, w_ref, out_ref, wide_ref, pick_ref):
    n = w_ref.shape[1]
    k = w_ref.shape[2]
    slots = back_ref.shape[0]
    lanes = GROUP * k
    step = pl.program_id(0)

    def gather(step, first, last):
        here = place_ref.at[pl.ds(step * lanes, lanes)]
        for i in range(first, last):
            row = pl.ds(here[i], 1)
            pick_ref[:, i : i + 1, :] = wide_ref[:, row, :]

    @pl.when(step == 0)
    def _():
        for t in range(slots // 256):
            rows = slice(256 * t, 256 * (t + 1))
            wide_ref[0, rows, :] = back_ref[rows, :128].astype(F32)
            wide_ref[1, rows, :] = back_ref[rows, 128:].astype(F32)
        wide_ref[:, slots:, :] = jnp.zeros_like(wide_ref[:, slots:, :])
        gather(step, 0, lanes)

    picked = jnp.concatenate([pick_ref[0], pick_ref[1]], axis=1).astype(BF16)
    for b in range(GROUP):
        rows = slice(b * n, (b + 1) * n)
        term = dot(w_ref[b], picked[b * k : (b + 1) * k, :])
        gather(step + 1, b * k, (b + 1) * k)
        out_ref[rows, :] = (solved_ref[rows, :].astype(F32) - term).astype(BF16)


def cost(flops, size):
    return pl.CostEstimate(flops=flops, bytes_accessed=size, transcendentals=0)


def shards(
    rhs_interior,
    rhs_interface,
    inv_blocks,
    coupling,
    interface_map,
    slot_counts,
    column_order,
    schur_inverse,
):
    f32, bf16 = F32, BF16
    nb, n = inv_blocks.shape[:2]
    k = coupling.shape[2]
    cols = rhs_interior.shape[1]
    owners = lax.axis_size(ALL)
    devs = lax.axis_size(DEV)
    secs = lax.axis_size(SEC)
    pairs = owners // 2
    slots = nb * k
    per_pair = slots // pairs
    half = per_pair // 2
    piece = rhs_interface.shape[0]
    pair_rows = 2 * piece
    band = piece * secs
    steps = nb // GROUP
    lanes = GROUP * k

    block_specs = [
        pl.BlockSpec((GROUP * n, cols), lambda i: (i, 0)),
        pl.BlockSpec((GROUP, n, n), lambda i: (i, 0, 0)),
    ]
    whole = pl.BlockSpec(memory_space=pltpu.VMEM)
    wire, place, index = pl.pallas_call(
        functools.partial(rank_kernel, (per_pair, half, pair_rows, pairs, owners)),
        in_specs=[pl.BlockSpec(memory_space=pltpu.SMEM), whole],
        out_specs=[whole, whole, whole],
        out_shape=[
            jax.ShapeDtypeStruct((steps + 1, lanes), jnp.int32),
            jax.ShapeDtypeStruct((steps + 1, lanes), jnp.int32),
            jax.ShapeDtypeStruct((pairs + pairs // 4, 256), f32),
        ],
        cost_estimate=cost(10**8, 10**5),
        name="rank",
    )(slot_counts, interface_map)
    sent = pl.pallas_call(
        functools.partial(forward_kernel, (half, pairs, devs)),
        grid_spec=pltpu.PrefetchScalarGridSpec(
            num_scalar_prefetch=1,
            grid=(steps,),
            in_specs=[
                pl.BlockSpec(index.shape, lambda i, at: (0, 0)),
                pl.BlockSpec((GROUP * n, cols), lambda i, at: (i, 0)),
                pl.BlockSpec((GROUP, n, n), lambda i, at: (i, 0, 0)),
                pl.BlockSpec((GROUP, None, k, n), lambda i, at: (i, 0, 0, 0)),
            ],
            out_specs=pl.BlockSpec((owners * WIRE, cols), lambda i, at: (0, 0)),
            scratch_shapes=[
                pltpu.VMEM((2, owners * WIRE + 8, 128), f32),
                pltpu.VMEM((2, lanes, 128), f32),
            ],
        ),
        out_shape=jax.ShapeDtypeStruct((owners * WIRE, cols), bf16),
        cost_estimate=cost(2 * 10**9, 14 * 10**6),
        name="forward",
    )(wire.reshape(-1), index, rhs_interior, inv_blocks, coupling)
    got = exchange(sent.reshape(owners, WIRE, cols), ALL)
    solved, weights = pl.pallas_call(
        middle_kernel,
        grid=(steps,),
        in_specs=[*block_specs, pl.BlockSpec((GROUP, None, k, n), lambda i: (i, 1, 0, 0))],
        out_specs=[
            pl.BlockSpec((GROUP * n, cols), lambda i: (i, 0)),
            pl.BlockSpec((GROUP, n, k), lambda i: (i, 0, 0)),
        ],
        out_shape=[
            jax.ShapeDtypeStruct((nb * n, cols), bf16),
            jax.ShapeDtypeStruct((nb, n, k), bf16),
        ],
        cost_estimate=cost(2 * 10**9, 20 * 10**6),
        name="middle",
    )(rhs_interior, inv_blocks, coupling)

    core = lax.axis_index("c")
    offs = jnp.where(core == 0, got[:, half, :half], got[:, half, half : 2 * half])
    target = jnp.pad(offs, ((0, 0), (0, WIRE - half)), constant_values=-1.0).reshape(1, -1)
    selector = jnp.arange(pair_rows, dtype=jnp.int32)[:, None].astype(bf16) == target
    arrived = jnp.dot(
        selector.astype(bf16), got.reshape(-1, cols), preferred_element_type=f32
    ).reshape(2, piece, cols)
    rhs_cols = jnp.take(rhs_interface, column_order, axis=1)
    mine = jnp.arange(2)[:, None, None] == core
    own = jnp.where(mine, rhs_cols[None], 0.0) - arrived
    reduced = own + lax.ppermute(own, "c", [(0, 1), (1, 0)])
    reduced = reduced.reshape(pair_rows, cols).astype(bf16)
    section = copies(reduced, "z").reshape(-1, cols)

    product = jnp.dot(schur_inverse, section, preferred_element_type=f32)
    parts = exchange(product.astype(bf16).reshape(secs, piece, cols), SEC)
    summed = jnp.sum(parts.astype(f32), axis=0).astype(bf16)
    values = copies(summed, SEC).reshape(band, cols)

    s = lax.axis_index(SEC)
    asked = lax.dynamic_slice_in_dim(got[:, half + 1 : half + 3], s * devs, devs, axis=0)
    asked = asked.reshape(devs, band // pair_rows, 64)[:, :, :per_pair]
    picker = asked[:, :, :, None] == jnp.arange(pair_rows, dtype=jnp.int32).astype(bf16)
    returned = jnp.einsum(
        "vjkr,jrn->vjkn",
        picker.astype(bf16),
        values.reshape(-1, pair_rows, cols),
        preferred_element_type=f32,
    ).astype(bf16)
    back = exchange(returned.reshape(devs, -1, cols), DEV).reshape(slots, cols)

    interior = pl.pallas_call(
        tail_kernel,
        grid_spec=pltpu.PrefetchScalarGridSpec(
            num_scalar_prefetch=1,
            grid=(steps,),
            in_specs=[
                pl.BlockSpec((slots, cols), lambda i, at: (0, 0)),
                pl.BlockSpec((GROUP * n, cols), lambda i, at: (i, 0)),
                pl.BlockSpec((GROUP, n, k), lambda i, at: (i, 0, 0)),
            ],
            out_specs=pl.BlockSpec((GROUP * n, cols), lambda i, at: (i, 0)),
            scratch_shapes=[
                pltpu.VMEM((2, slots + 8, 128), f32),
                pltpu.VMEM((2, lanes, 128), f32),
            ],
        ),
        out_shape=jax.ShapeDtypeStruct((nb * n, cols), bf16),
        cost_estimate=cost(4 * 10**9, 14 * 10**6),
        name="tail",
    )(place.reshape(-1), back, solved, weights)
    return interior, values.astype(f32)


def solution(mesh):
    fine = Mesh(mesh.devices.reshape(4, 4, 4, 2), ALL)
    placed = (
        P(ALL, None),
        P(ALL, None),
        P(ALL, None, None),
        P(ALL, None, None, None),
        P(ALL, None),
        P(ALL),
        P(),
        P(DEV, SEC),
    )
    return jax.shard_map(
        shards,
        mesh=fine,
        in_specs=placed,
        out_specs=(P(ALL, None), P(DEV, None)),
        check_vma=False,
    )
```

time: 143 us -> 138 us (0.965)
  Pallas kernels: 45.2 us -> 39.9 us
  waiting for transfers between devices: 36.1 us -> 38.3 us
  other arithmetic: 3.43 us -> 1.46 us
  local copies, waits for them, and re-layouts: 8.46 us -> 7.02 us
    pallas_call x2 -> x3, Pallas kernels: 33.4 us -> 28.1 us  [the longest x1 13.5 us: shards(): pl.pallas_call(functools.partial(forward_kernel, (half, pairs, devs)), gr...]
    all_to_all x3, waiting for transfers between devices: 35.1 us -> 37.2 us  [exchange(): return lax.all_to_all(blocks, axis, 0, 0, tiled=True)]
  transfers between devices with their start and end apart: 4 -> 4, of which waited for: 4 -> 4; matrix products, arithmetic and copies ran while one was open for 4% -> 3% of each run, Pallas kernels for 8% -> 9%
where the time goes in v3:
time: 138 us; the launch traced here: 136 us
  Pallas kernels  39.9 us (29%)
  waiting for transfers between devices  38.3 us (28%)
  starting transfers between devices  23.8 us (17%)
  blocking collectives  23.2 us (17%)
  local copies, waits for them, and re-layouts  7.02 us (5%)
  matrix products  1.82 us (1%)
  other arithmetic  1.46 us (1%)
    all_to_all x3, waiting for transfers between devices, exchange(): return lax.all_to_all(blocks, axis, 0, 0, tiled=True)  37.2 us
    all_to_all x2, blocking collectives, exchange(): return lax.all_to_all(blocks, axis, 0, 0, tiled=True)  23.2 us
    all_to_all x3, starting transfers between devices, exchange(): return lax.all_to_all(blocks, axis, 0, 0, tiled=True)  22.4 us
    pallas_call x1, Pallas kernels, shards(): pl.pallas_call(functools.partial(forward_kernel, (half, pairs, devs)), gr...  13.5 us
    pallas_call x1, Pallas kernels, shards(): pl.pallas_call(middle_kernel, grid=(steps,), in_specs=[*block_specs, pl.B...  11.8 us
    pallas_call x1, Pallas kernels, shards(): pl.pallas_call(tail_kernel, grid_spec=pltpu.PrefetchScalarGridSpec(num_sc...  11.5 us
    pallas_call x1, Pallas kernels, shards(): pl.pallas_call(functools.partial(rank_kernel, (per_pair, half, pair_rows,...  3.04 us
  transfers between devices with their start and end apart: 4, of which 4 were waited for; matrix products, arithmetic and copies ran while one was open for 3% of the time, Pallas kernels for 9%

profile of v3, /device:TPU:1, one launch (start us, length us, event | category | flops | bytes accessed | tf_op | source)
XLA Modules:
  0.0 136.3 jit_solution(8388860864573344050)
XLA Ops:
  0.6 0.0 copy-start
  0.6 3.0 %rank.1 = (s32[11,256]{1,0:T(8,128)}, s32[11,256]{1,0:T(8,128)}, f32[80,256]{1,0:T(8,128)}) custom-call(s32[40]{0:T(128)} %counts_ref.1, s32[40,64]{1,0:T(8,128)} %map_ref.1), custom_call_target="tpu_custom_call" | custom-call | flops 100000000 | bytes 100000 | tf_op jit(solution)/shard_map/rank/pallas_call | solution.py:203
  3.7 1.3 reshape.99.wire_ref
  5.0 13.5 %forward.1 = bf16[3072,256]{1,0:T(8,128)(2,1)} custom-call(s32[2816]{0:T(1024)} %reshape.99.wire_ref, f32[80,256]{1,0:T(8,128)} %get-tuple-element.9.index_ref, bf16[10240,256]{1,0:T(8,128)(2,1)} %rhs_ref.3, bf16[40,256,256]{2,1,0:T(8,128)(2,1)} %inv_ref.3, bf16[40,2,64,256]{3,2,1,0:T(8,128)(2,1)} %couple_ref.3), custom_call_target="tpu_custom_call" | custom-call | flops 2000000000 | bytes 14000000 | tf_op jit(solution)/shard_map/forward/pallas_call | solution.py:215
  18.5 0.0 copy-start.2
  18.5 0.0 copy-start.4
  18.5 11.5 %all-to-all-start = ((bf16[128,24,256]{2,1,0:T(8,128)(2,1)}), bf16[128,24,256]{2,1,0:T(8,128)(2,1)S(1)}, u32[]{:S(2)}, u32[]{:S(2)}) async-start(bf16[128,24,256]{2,1,0:T(8,128)(2,1)} %bitcast.30), calls=%async_computation | async-start | bytes 3145728 | tf_op jit(solution)/shard_map/all_to_all | solution.py:20
  30.0 0.0 copy-done.2
  30.0 0.1 copy.21
  30.1 0.0 copy-done.4
  30.1 0.7 gather_fusion
  30.9 0.1 select_bitcast_fusion
  31.0 0.1 copy.22
  31.1 23.4 %all-to-all-done = bf16[128,24,256]{2,1,0:T(8,128)(2,1)S(1)} async-done(((bf16[128,24,256]{2,1,0:T(8,128)(2,1)}), bf16[128,24,256]{2,1,0:T(8,128)(2,1)S(1)}, u32[]{:S(2)}, u32[]{:S(2)}) %all-to-all-start) | async-done | bytes 1572896 | tf_op jit(solution)/shard_map/all_to_all | solution.py:20
  54.5 0.0 copy-start.1
  54.5 0.2 fusion.18
  54.7 0.1 copy.30
  54.8 0.1 copy.31
  54.9 0.1 copy.32
  55.1 0.1 eq.51
  55.2 0.5 fusion.11
  55.7 1.4 %collective-permute-start = (f32[2,80,256]{2,1,0:T(8,128)S(1)}, f32[2,80,256]{2,1,0:T(8,128)S(1)}, u32[]{:S(2)}, u32[]{:S(2)}) collective-permute-start(f32[2,80,256]{2,1,0:T(8,128)S(1)} %fusion.11), channel_id=1, source_target_pairs={{0,1},{1,0},{2,3},{3,2},{4,5},{5,4},{6,7},{7,6},{8,9},{9,8},{10,11... | collective-permute-start | bytes 491528 | tf_op jit(solution)/shard_map/ppermute | solution.py:263
  57.1 1.0 collective-permute-done
  58.2 0.0 copy-done.1
  58.2 9.2 %all_to_all.25 = bf16[4,160,256]{2,1,0:T(8,128)(2,1)S(1)} all-to-all(bf16[4,160,256]{2,1,0:T(8,128)(2,1)S(1)} %broadcast_in_dim.55), channel_id=1, replica_groups=mesh['y'=4,'x'=4,'z'=4,'c'=2] {'z'}, dimensions={0} | all-to-all | bytes 655360 | tf_op jit(solution)/shard_map/all_to_all | solution.py:20
  67.4 0.0 copy-done
  67.4 0.7 fusion.2
  68.1 0.2 copy.26
  68.4 14.0 %all_to_all.26 = bf16[16,80,256]{2,1,0:T(8,128)(2,1)S(1)} all-to-all(bf16[16,80,256]{2,1,0:T(8,128)(2,1)S(1)} %bitcast.31), channel_id=1, replica_groups=mesh['y'=4,'x'=4,'z'=4,'c'=2] {'y','x'}, dimensions={0} | all-to-all | bytes 1310720 | tf_op jit(solution)/shard_map/all_to_all | solution.py:20
  82.4 0.1 reduce_sum.12
  82.5 0.9 broadcast_in_dim.56
  83.4 3.6 %all-to-all-start.3 = ((bf16[16,80,256]{2,1,0:T(8,128)(2,1)}), bf16[16,80,256]{2,1,0:T(8,128)(2,1)S(1)}, u32[]{:S(2)}, u32[]{:S(2)}) async-start(bf16[16,80,256]{2,1,0:T(8,128)(2,1)} %broadcast_in_dim.56), calls=%async_computation.3 | async-start | bytes 1310720 | tf_op jit(solution)/shard_map/all_to_all | solution.py:20
  87.0 1.2 slice.20
  88.2 0.1 reshape.104
  88.3 9.5 %all-to-all-done.3 = bf16[16,80,256]{2,1,0:T(8,128)(2,1)S(1)} async-done(((bf16[16,80,256]{2,1,0:T(8,128)(2,1)}), bf16[16,80,256]{2,1,0:T(8,128)(2,1)S(1)}, u32[]{:S(2)}, u32[]{:S(2)}) %all-to-all-start.3) | async-done | bytes 655392 | tf_op jit(solution)/shard_map/all_to_all | solution.py:20
  97.8 0.6 fusion.8
  98.5 1.1 copy.28
  99.6 0.0 copy-start.3
  99.6 7.3 %all-to-all-start.4 = ((bf16[8,320,256]{2,1,0:T(8,128)(2,1)}), bf16[8,320,256]{2,1,0:T(8,128)(2,1)}, u32[]{:S(2)}, u32[]{:S(2)}) async-start(bf16[8,320,256]{2,1,0:T(8,128)(2,1)} %bitcast.13), calls=%async_computation.4 | async-start | bytes 2621440 | tf_op jit(solution)/shard_map/all_to_all | solution.py:20
  106.9 0.0 copy-done.3
  106.9 0.6 reshape.98.place_ref
  107.5 11.8 %middle.1 = (bf16[10240,256]{1,0:T(8,128)(2,1)}, bf16[40,256,64]{2,1,0:T(8,128)(2,1)}) custom-call(bf16[10240,256]{1,0:T(8,128)(2,1)} %rhs_ref.3, bf16[40,256,256]{2,1,0:T(8,128)(2,1)} %inv_ref.3, bf16[40,2,64,256]{3,2,1,0:T(8,128)(2,1)} %couple_ref.3), custom_call_target="tpu_custom_call" | custom-call | flops 2000000000 | bytes 20000000 | tf_op jit(solution)/shard_map/middle/pallas_call | solution.py:237
  119.4 1.2 bitcast_convert_fusion
  120.6 4.3 %all-to-all-done.4 = bf16[8,320,256]{2,1,0:T(8,128)(2,1)} async-done(((bf16[8,320,256]{2,1,0:T(8,128)(2,1)}), bf16[8,320,256]{2,1,0:T(8,128)(2,1)}, u32[]{:S(2)}, u32[]{:S(2)}) %all-to-all-start.4) | async-done | bytes 1310752 | tf_op jit(solution)/shard_map/all_to_all | solution.py:20
  124.8 11.5 %tail.1 = bf16[10240,256]{1,0:T(8,128)(2,1)} custom-call(s32[2816]{0:T(1024)} %reshape.98.place_ref, bf16[2560,256]{1,0:T(8,128)(2,1)} %bitcast.14.back_ref, bf16[10240,256]{1,0:T(8,128)(2,1)} %get-tuple-element.10.solved_ref, bf16[40,256,64]{2,1,0:T(8,128)(2,1)} %get-tuple-element.11.w_ref), custom_call_target="tpu_custom_call" | custom-call | flops 4000000000 | bytes 14000000 | tf_op jit(solution)/shard_map/tail/pallas_call | solution.py:284
  (12 shorter events, 0.1 us)
Async XLA Ops:
  0.6 66.8 %copy-start = (bf16[1280,640]{1,0:T(8,128)(2,1)S(1)}, bf16[1280,640]{1,0:T(8,128)(2,1)}, u32[]{:S(2)}) copy-start(bf16[1280,640]{1,0:T(8,128)(2,1)} %param.15) | copy-start | bytes 4915204
  18.5 11.5 %copy-start.2 = (f32[80,256]{1,0:T(8,128)S(1)}, f32[80,256]{1,0:T(8,128)}, u32[]{:S(2)}) copy-start(f32[80,256]{1,0:T(8,128)} %param.9) | copy-start | bytes 245764
  18.5 11.6 %copy-start.4 = (s32[256]{0:T(256)S(1)}, s32[256]{0:T(256)}, u32[]{:S(2)}) copy-start(s32[256]{0:T(256)} %param.14) | copy-start | bytes 3076
  18.5 36.0 %all-to-all-start = ((bf16[128,24,256]{2,1,0:T(8,128)(2,1)}), bf16[128,24,256]{2,1,0:T(8,128)(2,1)S(1)}, u32[]{:S(2)}, u32[]{:S(2)}) async-start(bf16[128,24,256]{2,1,0:T(8,128)(2,1)} %bitcast.30), calls=%async_computation | async-start | bytes 3145728 | tf_op jit(solution)/shard_map/all_to_all | solution.py:20
  54.5 3.6 %copy-start.1 = (bf16[128,24,256]{2,1,0:T(8,128)(2,1)}, bf16[128,24,256]{2,1,0:T(8,128)(2,1)S(1)}, u32[]{:S(2)}) copy-start(bf16[128,24,256]{2,1,0:T(8,128)(2,1)S(1)} %all-to-all-done) | copy-start | bytes 4718596
  55.7 2.5 %collective-permute-start = (f32[2,80,256]{2,1,0:T(8,128)S(1)}, f32[2,80,256]{2,1,0:T(8,128)S(1)}, u32[]{:S(2)}, u32[]{:S(2)}) collective-permute-start(f32[2,80,256]{2,1,0:T(8,128)S(1)} %fusion.11), channel_id=1, source_target_pairs={{0,1},{1,0},{2,3},{3,2},{4,5},{5,4},{6,7},{7,6},{8,9},{9,8},{10,11... | collective-permute-start | bytes 491528 | tf_op jit(solution)/shard_map/ppermute | solution.py:263
  83.4 14.5 %all-to-all-start.3 = ((bf16[16,80,256]{2,1,0:T(8,128)(2,1)}), bf16[16,80,256]{2,1,0:T(8,128)(2,1)S(1)}, u32[]{:S(2)}, u32[]{:S(2)}) async-start(bf16[16,80,256]{2,1,0:T(8,128)(2,1)} %broadcast_in_dim.56), calls=%async_computation.3 | async-start | bytes 1310720 | tf_op jit(solution)/shard_map/all_to_all | solution.py:20
  99.6 7.3 %copy-start.3 = (s32[11,256]{1,0:T(8,128)S(1)}, s32[11,256]{1,0:T(8,128)}, u32[]{:S(2)}) copy-start(s32[11,256]{1,0:T(8,128)} %get-tuple-element.7) | copy-start | bytes 33796
  99.6 25.2 %all-to-all-start.4 = ((bf16[8,320,256]{2,1,0:T(8,128)(2,1)}), bf16[8,320,256]{2,1,0:T(8,128)(2,1)}, u32[]{:S(2)}, u32[]{:S(2)}) async-start(bf16[8,320,256]{2,1,0:T(8,128)(2,1)} %bitcast.13), calls=%async_computation.4 | async-start | bytes 2621440 | tf_op jit(solution)/shard_map/all_to_all | solution.py:20

commit v4 on v3

v4 whole, which is shorter than its diff:
```python
import functools

import jax
import jax.numpy as jnp
from jax import lax
from jax.experimental import pallas as pl
from jax.experimental.pallas import tpu as pltpu
from jax.sharding import Mesh
from jax.sharding import PartitionSpec as P

ALL = ("y", "x", "z", "c")
SEC = ("y", "x")
DEV = ("z", "c")
WIRE = 24
GROUP = 4
F32, BF16 = jnp.float32, jnp.bfloat16


def exchange(blocks, axis):
    return lax.all_to_all(blocks, axis, 0, 0, tiled=True)


def copies(array, axis):
    size = lax.axis_size(axis)
    return exchange(jnp.broadcast_to(array[None], (size, *array.shape)), axis)


def iota(shape, dim):
    return lax.broadcasted_iota(jnp.int32, shape, dim).astype(F32)


def quotient(x, n):
    return jnp.floor((x + 0.5) * (1.0 / n))


def dot(a, b, dims=((1,), (0,))):
    return lax.dot_general(a, b, (dims, ((), ())), preferred_element_type=F32)


def onehot(mask):
    return jnp.where(mask, 1.0, 0.0).astype(BF16)


def forward_kernel(
    sizes, counts_ref, map_ref, rhs_ref, inv_ref, couple_ref, out_ref, place_ref,
    wide_ref, stage_ref, base_ref, offs_ref, wire_ref, at_ref, sem
):
    per_pair, half, pair_rows, pairs, devs = sizes
    step = pl.program_id(0)
    n = inv_ref.shape[1]
    k = couple_ref.shape[1]
    lanes = GROUP * k
    rows_out = out_ref.shape[0]
    now, before = lax.rem(step, 2), lax.rem(step + 1, 2)

    def handover(slot):
        return pltpu.make_async_copy(wire_ref.at[slot], at_ref.at[slot], sem.at[slot])

    @pl.when(step == 0)
    def _():
        stage_ref[...] = jnp.zeros_like(stage_ref)
        base_ref[...] = jnp.zeros_like(base_ref)
        offs_ref[...] = jnp.zeros_like(offs_ref)
        for i in range(lanes):
            at_ref[1, 0, i] = rows_out

    @pl.when(step > 0)
    def _():
        handover(before).wait()

    slot = jnp.concatenate(
        [map_ref[pl.ds(step * GROUP + b, 1), :] for b in range(GROUP)], axis=1
    ).astype(F32)
    at = lax.broadcasted_iota(jnp.int32, (1, k), 1)
    live = jnp.concatenate(
        [jnp.where(at < counts_ref[step * GROUP + b], 1.0, 0.0) for b in range(GROUP)], axis=1
    )
    pair = quotient(slot, pair_rows)
    off = slot - pair_rows * pair
    table = jnp.where(iota((pairs, lanes), 0) == pair, 1.0, 0.0)
    earlier = dot(
        table.astype(BF16), onehot(iota((lanes, lanes), 0) < iota((lanes, lanes), 1))
    )
    rank = jnp.sum(table * (earlier + base_ref[:, :1]), axis=0, keepdims=True)
    base_ref[...] += jnp.sum(table, axis=1, keepdims=True)
    place = pair * per_pair + rank
    place_ref[0] = jnp.where(live == 0.0, pairs * per_pair, place).astype(jnp.int32)
    wire = place + (WIRE - half) * quotient(place, half)
    wire_ref[now] = wire.astype(jnp.int32)
    handover(now).start()
    row64 = (lax.broadcasted_iota(jnp.int32, (256, lanes), 0) & 63).astype(F32)
    offs_ref[...] += dot((table * off).astype(BF16), onehot(row64 == rank), ((1,), (1,)))

    def move(slot, first, last):
        for i in range(first, last):
            row = pl.ds(at_ref[slot, 0, i], 1)
            wide_ref[:, row, :] = stage_ref[:, i : i + 1, :]

    solved = [
        dot(inv_ref[b], rhs_ref[b * n : (b + 1) * n, :]).astype(BF16) for b in range(GROUP)
    ]
    move(before, 0, lanes // 2)
    parts = [dot(couple_ref[b], solved[b]) for b in range(GROUP)]
    move(before, lanes // 2, lanes)
    depth = lax.broadcasted_iota(jnp.int32, (k, 2 * 128), 0)
    for b in range(GROUP):
        own = slice(b * k, (b + 1) * k)
        part = jnp.where(depth < counts_ref[step * GROUP + b], parts[b], 0.0)
        stage_ref[0, own, :] = part[:, :128]
        stage_ref[1, own, :] = part[:, 128:]

    @pl.when(step == pl.num_programs(0) - 1)
    def _():
        handover(now).wait()
        move(now, 0, lanes)
        offs = offs_ref[...]
        p = lax.broadcasted_iota(jnp.int32, offs.shape, 0)
        lane = lax.broadcasted_iota(jnp.int32, offs.shape, 1)
        spread = jnp.where((lane >> 6) == (p & 3), offs, 0.0).astype(BF16)
        groups = pairs // 4
        member = iota((groups, pairs), 0) == quotient(iota((groups, pairs), 1), 4)
        wanted = dot(onehot(member), spread)
        level = lax.broadcasted_iota(jnp.int32, (WIRE - half, 128), 0)
        for h in range(2):
            cut = slice(128 * h, 128 * (h + 1))
            for v in range(devs):
                one = jnp.broadcast_to(wanted[2 * v : 2 * v + 1, cut], level.shape)
                two = jnp.broadcast_to(wanted[2 * v + 1 : 2 * v + 2, cut], level.shape)
                tail = jnp.where(level == 1, one, jnp.where(level == 2, two, 0.0))
                for d in range(v, rows_out // WIRE, devs):
                    own = jnp.broadcast_to(offs_ref[d // 2 : d // 2 + 1, cut], level.shape)
                    w = d * WIRE + half
                    wide_ref[h, w : w + WIRE - half, :] = jnp.where(level == 0, own, tail)
        for t in range(rows_out // 256):
            rows = slice(256 * t, 256 * (t + 1))
            out_ref[rows, :128] = wide_ref[0, rows, :].astype(BF16)
            out_ref[rows, 128:] = wide_ref[1, rows, :].astype(BF16)


def middle_kernel(rhs_ref, inv_ref, couple_ref, solved_ref, w_ref):
    n = inv_ref.shape[1]
    for b in range(GROUP):
        rows = slice(b * n, (b + 1) * n)
        solved_ref[rows, :] = dot(inv_ref[b], rhs_ref[rows, :]).astype(BF16)
    for b in range(0, GROUP, 2):
        w_ref[b // 2] = jnp.concatenate(
            [dot(inv_ref[c], couple_ref[c], ((1,), (1,))) for c in (b, b + 1)], axis=1
        ).astype(BF16)


def tail_kernel(place_ref, back_ref, solved_ref, w_ref, out_ref, wide_ref, pick_ref):
    n = w_ref.shape[1]
    k = w_ref.shape[2] // 2
    slots = back_ref.shape[0]
    lanes = GROUP * k
    step = pl.program_id(0)

    def gather(step, first, last):
        here = place_ref.at[pl.ds(step * lanes, lanes)]
        for i in range(first, last):
            row = pl.ds(here[i], 1)
            pick_ref[:, i : i + 1, :] = wide_ref[:, row, :]

    @pl.when(step == 0)
    def _():
        for t in range(slots // 256):
            rows = slice(256 * t, 256 * (t + 1))
            wide_ref[0, rows, :] = back_ref[rows, :128].astype(F32)
            wide_ref[1, rows, :] = back_ref[rows, 128:].astype(F32)
        wide_ref[:, slots:, :] = jnp.zeros_like(wide_ref[:, slots:, :])
        gather(step, 0, lanes)

    picked = jnp.concatenate([pick_ref[0], pick_ref[1]], axis=1).astype(BF16)
    empty = jnp.zeros((k, picked.shape[1]), BF16)
    for b in range(GROUP):
        rows = slice(b * n, (b + 1) * n)
        own = picked[b * k : (b + 1) * k, :]
        pad = [own, empty] if b % 2 == 0 else [empty, own]
        term = dot(w_ref[b // 2], jnp.concatenate(pad, axis=0))
        gather(step + 1, b * k, (b + 1) * k)
        out_ref[rows, :] = (solved_ref[rows, :].astype(F32) - term).astype(BF16)


def cost(flops, size):
    return pl.CostEstimate(flops=flops, bytes_accessed=size, transcendentals=0)


def shards(
    rhs_interior,
    rhs_interface,
    inv_blocks,
    coupling,
    interface_map,
    slot_counts,
    column_order,
    schur_inverse,
):
    f32, bf16 = F32, BF16
    nb, n = inv_blocks.shape[:2]
    k = coupling.shape[2]
    cols = rhs_interior.shape[1]
    owners = lax.axis_size(ALL)
    devs = lax.axis_size(DEV)
    secs = lax.axis_size(SEC)
    pairs = owners // 2
    slots = nb * k
    per_pair = slots // pairs
    half = per_pair // 2
    piece = rhs_interface.shape[0]
    pair_rows = 2 * piece
    band = piece * secs
    steps = nb // GROUP
    lanes = GROUP * k

    block_specs = [
        pl.BlockSpec((GROUP * n, cols), lambda i: (i, 0)),
        pl.BlockSpec((GROUP, n, n), lambda i: (i, 0, 0)),
    ]
    sent, place = pl.pallas_call(
        functools.partial(forward_kernel, (per_pair, half, pair_rows, pairs, devs)),
        grid_spec=pltpu.PrefetchScalarGridSpec(
            num_scalar_prefetch=1,
            grid=(steps,),
            in_specs=[
                pl.BlockSpec((nb, k), lambda i, at: (0, 0)),
                pl.BlockSpec((GROUP * n, cols), lambda i, at: (i, 0)),
                pl.BlockSpec((GROUP, n, n), lambda i, at: (i, 0, 0)),
                pl.BlockSpec((GROUP, None, k, n), lambda i, at: (i, 0, 0, 0)),
            ],
            out_specs=[
                pl.BlockSpec((owners * WIRE, cols), lambda i, at: (0, 0)),
                pl.BlockSpec((1, 1, lanes), lambda i, at: (i, 0, 0)),
            ],
            scratch_shapes=[
                pltpu.VMEM((2, owners * WIRE + 8, 128), f32),
                pltpu.VMEM((2, lanes, 128), f32),
                pltpu.VMEM((pairs, 128), f32),
                pltpu.VMEM((pairs, 256), f32),
                pltpu.VMEM((2, 1, lanes), jnp.int32),
                pltpu.SMEM((2, 1, lanes), jnp.int32),
                pltpu.SemaphoreType.DMA((2,)),
            ],
        ),
        out_shape=[
            jax.ShapeDtypeStruct((owners * WIRE, cols), bf16),
            jax.ShapeDtypeStruct((steps, 1, lanes), jnp.int32),
        ],
        cost_estimate=cost(2 * 10**9, 14 * 10**6),
        name="forward",
    )(slot_counts, interface_map, rhs_interior, inv_blocks, coupling)
    got = exchange(sent.reshape(owners, WIRE, cols), ALL)
    solved, weights = pl.pallas_call(
        middle_kernel,
        grid=(steps,),
        in_specs=[*block_specs, pl.BlockSpec((GROUP, None, k, n), lambda i: (i, 1, 0, 0))],
        out_specs=[
            pl.BlockSpec((GROUP * n, cols), lambda i: (i, 0)),
            pl.BlockSpec((GROUP // 2, n, 2 * k), lambda i: (i, 0, 0)),
        ],
        out_shape=[
            jax.ShapeDtypeStruct((nb * n, cols), bf16),
            jax.ShapeDtypeStruct((nb // 2, n, 2 * k), bf16),
        ],
        cost_estimate=cost(2 * 10**9, 20 * 10**6),
        name="middle",
    )(rhs_interior, inv_blocks, coupling)

    core = lax.axis_index("c")
    offs = jnp.where(core == 0, got[:, half, :half], got[:, half, half : 2 * half])
    offs, solved, weights = lax.optimization_barrier((offs, solved, weights))
    target = jnp.pad(offs, ((0, 0), (0, WIRE - half)), constant_values=-1.0).reshape(1, -1)
    selector = jnp.arange(pair_rows, dtype=jnp.int32)[:, None].astype(bf16) == target
    arrived = jnp.dot(
        selector.astype(bf16), got.reshape(-1, cols), preferred_element_type=f32
    ).reshape(2, piece, cols)
    rhs_cols = jnp.take(rhs_interface, column_order, axis=1)
    mine = jnp.arange(2)[:, None, None] == core
    own = jnp.where(mine, rhs_cols[None], 0.0) - arrived
    reduced = own + lax.ppermute(own, "c", [(0, 1), (1, 0)])
    reduced = reduced.reshape(pair_rows, cols).astype(bf16)
    section = copies(reduced, "z").reshape(-1, cols)

    product = jnp.dot(schur_inverse, section, preferred_element_type=f32)
    parts = exchange(product.astype(bf16).reshape(secs, piece, cols), SEC)
    summed = jnp.sum(parts.astype(f32), axis=0).astype(bf16)
    values = copies(summed, SEC).reshape(band, cols)

    s = lax.axis_index(SEC)
    asked = lax.dynamic_slice_in_dim(got[:, half + 1 : half + 3], s * devs, devs, axis=0)
    asked = asked.reshape(devs, band // pair_rows, 64)[:, :, :per_pair]
    picker = asked[:, :, :, None] == jnp.arange(pair_rows, dtype=jnp.int32).astype(bf16)
    returned = jnp.einsum(
        "vjkr,jrn->vjkn",
        picker.astype(bf16),
        values.reshape(-1, pair_rows, cols),
        preferred_element_type=f32,
    ).astype(bf16)
    back = exchange(returned.reshape(devs, -1, cols), DEV).reshape(slots, cols)

    interior = pl.pallas_call(
        tail_kernel,
        grid_spec=pltpu.PrefetchScalarGridSpec(
            num_scalar_prefetch=1,
            grid=(steps,),
            in_specs=[
                pl.BlockSpec((slots, cols), lambda i, at: (0, 0)),
                pl.BlockSpec((GROUP * n, cols), lambda i, at: (i, 0)),
                pl.BlockSpec((GROUP // 2, n, 2 * k), lambda i, at: (i, 0, 0)),
            ],
            out_specs=pl.BlockSpec((GROUP * n, cols), lambda i, at: (i, 0)),
            scratch_shapes=[
                pltpu.VMEM((2, slots + 8, 128), f32),
                pltpu.VMEM((2, lanes, 128), f32),
            ],
        ),
        out_shape=jax.ShapeDtypeStruct((nb * n, cols), bf16),
        cost_estimate=cost(4 * 10**9, 14 * 10**6),
        name="tail",
    )(jnp.pad(place.reshape(-1), (0, lanes), constant_values=slots), back, solved, weights)
    return interior, values.astype(f32)


def solution(mesh):
    fine = Mesh(mesh.devices.reshape(4, 4, 4, 2), ALL)
    placed = (
        P(ALL, None),
        P(ALL, None),
        P(ALL, None, None),
        P(ALL, None, None, None),
        P(ALL, None),
        P(ALL),
        P(),
        P(DEV, SEC),
    )
    return jax.shard_map(
        shards,
        mesh=fine,
        in_specs=placed,
        out_specs=(P(ALL, None), P(DEV, None)),
        check_vma=False,
    )
```

time: 138 us -> 134 us (0.971)
  Pallas kernels: 39.9 us -> 36.4 us
    pallas_call x2 -> x1, Pallas kernels: 16.5 us -> 14.6 us  [shards(): pl.pallas_call(functools.partial(forward_kernel, (per_pair, half, pair_ro...]
  transfers between devices with their start and end apart: 4 -> 4, of which waited for: 4 -> 4; matrix products, arithmetic and copies ran while one was open for 3% -> 3% of each run, Pallas kernels for 9% -> 8%
where the time goes in v4:
time: 134 us; the launch traced here: 133 us
  waiting for transfers between devices  39.5 us (29%)
  Pallas kernels  36.4 us (27%)
  starting transfers between devices  23.8 us (18%)
  blocking collectives  23.2 us (17%)
  local copies, waits for them, and re-layouts  5.72 us (4%)
  matrix products  1.83 us (1%)
  other arithmetic  1.49 us (1%)
    all_to_all x3, waiting for transfers between devices, exchange(): return lax.all_to_all(blocks, axis, 0, 0, tiled=True)  38.5 us
    all_to_all x2, blocking collectives, exchange(): return lax.all_to_all(blocks, axis, 0, 0, tiled=True)  23.2 us
    all_to_all x3, starting transfers between devices, exchange(): return lax.all_to_all(blocks, axis, 0, 0, tiled=True)  22.4 us
    pallas_call x1, Pallas kernels, shards(): pl.pallas_call(functools.partial(forward_kernel, (per_pair, half, pair_ro...  14.6 us
    pallas_call x1, Pallas kernels, shards(): pl.pallas_call(tail_kernel, grid_spec=pltpu.PrefetchScalarGridSpec(num_sc...  11.2 us
    pallas_call x1, Pallas kernels, shards(): pl.pallas_call(middle_kernel, grid=(steps,), in_specs=[*block_specs, pl.B...  10.6 us
  transfers between devices with their start and end apart: 4, of which 4 were waited for; matrix products, arithmetic and copies ran while one was open for 3% of the time, Pallas kernels for 8%

profile of v4, /device:TPU:1, one launch (start us, length us, event | category | flops | bytes accessed | tf_op | source)
XLA Modules:
  0.0 132.8 jit_solution(14282970631764125305)
XLA Ops:
  0.6 0.0 copy-start
  0.6 14.6 %forward.1 = (bf16[3072,256]{1,0:T(8,128)(2,1)}, s32[10,1,256]{2,1,0:T(1,128)}) custom-call(s32[40]{0:T(128)} %counts_ref.1, s32[40,64]{1,0:T(8,128)} %map_ref.1, bf16[10240,256]{1,0:T(8,128)(2,1)} %rhs_ref.3, bf16[40,256,256]{2,1,0:T(8,128)(2,1)} %inv_ref.3, bf16[40,2,64,256]{3,2,1,0:T(8,128)(2,1)} %couple_ref.3), custom_call_target="tpu_custom_call" | custom-call | flops 2000000000 | bytes 14000000 | tf_op jit(solution)/shard_map/forward/pallas_call | solution.py:219
  15.3 0.0 copy-start.2
  15.3 0.0 copy-start.4
  15.3 11.5 %all-to-all-start = ((bf16[128,24,256]{2,1,0:T(8,128)(2,1)}), bf16[128,24,256]{2,1,0:T(8,128)(2,1)S(1)}, u32[]{:S(2)}, u32[]{:S(2)}) async-start(bf16[128,24,256]{2,1,0:T(8,128)(2,1)} %bitcast.33), calls=%async_computation | async-start | bytes 3145728 | tf_op jit(solution)/shard_map/all_to_all | solution.py:20
  26.8 0.0 copy-done.2
  26.8 0.1 copy.21
  26.9 0.0 copy-done.4
  27.0 0.7 gather_fusion
  27.7 0.1 select_bitcast_fusion
  27.8 0.1 copy.22
  27.9 10.6 %middle.1 = (bf16[10240,256]{1,0:T(8,128)(2,1)}, bf16[20,256,128]{2,1,0:T(8,128)(2,1)}) custom-call(bf16[10240,256]{1,0:T(8,128)(2,1)} %rhs_ref.3, bf16[40,256,256]{2,1,0:T(8,128)(2,1)} %inv_ref.3, bf16[40,2,64,256]{3,2,1,0:T(8,128)(2,1)} %couple_ref.3), custom_call_target="tpu_custom_call" | custom-call | flops 2000000000 | bytes 20000000 | tf_op jit(solution)/shard_map/middle/pallas_call | solution.py:252
  38.5 12.8 %all-to-all-done = bf16[128,24,256]{2,1,0:T(8,128)(2,1)S(1)} async-done(((bf16[128,24,256]{2,1,0:T(8,128)(2,1)}), bf16[128,24,256]{2,1,0:T(8,128)(2,1)S(1)}, u32[]{:S(2)}, u32[]{:S(2)}) %all-to-all-start) | async-done | bytes 1572896 | tf_op jit(solution)/shard_map/all_to_all | solution.py:20
  51.4 0.0 copy-start.1
  51.4 0.2 fusion.18
  51.5 0.1 copy.31
  51.6 0.1 copy.30
  51.7 0.1 copy.32
  51.9 0.1 eq.51
  52.0 0.5 fusion.11
  52.5 1.4 %collective-permute-start = (f32[2,80,256]{2,1,0:T(8,128)S(1)}, f32[2,80,256]{2,1,0:T(8,128)S(1)}, u32[]{:S(2)}, u32[]{:S(2)}) collective-permute-start(f32[2,80,256]{2,1,0:T(8,128)S(1)} %fusion.11), channel_id=1, source_target_pairs={{0,1},{1,0},{2,3},{3,2},{4,5},{5,4},{6,7},{7,6},{8,9},{9,8},{10,11... | collective-permute-start | bytes 491528 | tf_op jit(solution)/shard_map/ppermute | solution.py:279
  53.9 1.0 collective-permute-done
  55.0 0.0 copy-done.1
  55.0 9.2 %all_to_all.25 = bf16[4,160,256]{2,1,0:T(8,128)(2,1)S(1)} all-to-all(bf16[4,160,256]{2,1,0:T(8,128)(2,1)S(1)} %broadcast_in_dim.55), channel_id=1, replica_groups=mesh['y'=4,'x'=4,'z'=4,'c'=2] {'z'}, dimensions={0} | all-to-all | bytes 655360 | tf_op jit(solution)/shard_map/all_to_all | solution.py:20
  64.2 0.0 copy-done
  64.2 0.7 fusion.2
  65.0 0.2 copy.26
  65.2 14.0 %all_to_all.26 = bf16[16,80,256]{2,1,0:T(8,128)(2,1)S(1)} all-to-all(bf16[16,80,256]{2,1,0:T(8,128)(2,1)S(1)} %bitcast.30), channel_id=1, replica_groups=mesh['y'=4,'x'=4,'z'=4,'c'=2] {'y','x'}, dimensions={0} | all-to-all | bytes 1310720 | tf_op jit(solution)/shard_map/all_to_all | solution.py:20
  79.2 0.1 reduce_sum.12
  79.3 0.9 broadcast_in_dim.56
  80.2 3.6 %all-to-all-start.3 = ((bf16[16,80,256]{2,1,0:T(8,128)(2,1)}), bf16[16,80,256]{2,1,0:T(8,128)(2,1)S(1)}, u32[]{:S(2)}, u32[]{:S(2)}) async-start(bf16[16,80,256]{2,1,0:T(8,128)(2,1)} %broadcast_in_dim.56), calls=%async_computation.3 | async-start | bytes 1310720 | tf_op jit(solution)/shard_map/all_to_all | solution.py:20
  83.8 1.2 slice.20
  85.0 0.1 reshape.100
  85.1 9.5 %all-to-all-done.3 = bf16[16,80,256]{2,1,0:T(8,128)(2,1)S(1)} async-done(((bf16[16,80,256]{2,1,0:T(8,128)(2,1)}), bf16[16,80,256]{2,1,0:T(8,128)(2,1)S(1)}, u32[]{:S(2)}, u32[]{:S(2)}) %all-to-all-start.3) | async-done | bytes 655392 | tf_op jit(solution)/shard_map/all_to_all | solution.py:20
  94.7 0.6 fusion.8
  95.3 1.1 copy.28
  96.4 0.0 copy-start.3
  96.4 7.3 %all-to-all-start.4 = ((bf16[8,320,256]{2,1,0:T(8,128)(2,1)}), bf16[8,320,256]{2,1,0:T(8,128)(2,1)}, u32[]{:S(2)}, u32[]{:S(2)}) async-start(bf16[8,320,256]{2,1,0:T(8,128)(2,1)} %bitcast.13), calls=%async_computation.4 | async-start | bytes 2621440 | tf_op jit(solution)/shard_map/all_to_all | solution.py:20
  103.8 0.0 copy-done.3
  103.8 0.6 pad.8.place_ref
  104.4 1.2 bitcast_convert_fusion
  105.6 16.1 %all-to-all-done.4 = bf16[8,320,256]{2,1,0:T(8,128)(2,1)} async-done(((bf16[8,320,256]{2,1,0:T(8,128)(2,1)}), bf16[8,320,256]{2,1,0:T(8,128)(2,1)}, u32[]{:S(2)}, u32[]{:S(2)}) %all-to-all-start.4) | async-done | bytes 1310752 | tf_op jit(solution)/shard_map/all_to_all | solution.py:20
  121.7 11.2 %tail.1 = bf16[10240,256]{1,0:T(8,128)(2,1)} custom-call(s32[2816]{0:T(1024)} %pad.8.place_ref, bf16[2560,256]{1,0:T(8,128)(2,1)} %bitcast.14.back_ref, bf16[10240,256]{1,0:T(8,128)(2,1)} %get-tuple-element.14.solved_ref, bf16[20,256,128]{2,1,0:T(8,128)(2,1)} %get-tuple-element.15.w_ref), custom_call_target="tpu_custom_call" | custom-call | flops 4000000000 | bytes 14000000 | tf_op jit(solution)/shard_map/tail/pallas_call | solution.py:300
  (14 shorter events, 0.2 us)
Async XLA Ops:
  0.6 63.6 %copy-start = (bf16[1280,640]{1,0:T(8,128)(2,1)S(1)}, bf16[1280,640]{1,0:T(8,128)(2,1)}, u32[]{:S(2)}) copy-start(bf16[1280,640]{1,0:T(8,128)(2,1)} %param.15) | copy-start | bytes 4915204
  15.3 11.5 %copy-start.2 = (f32[80,256]{1,0:T(8,128)S(1)}, f32[80,256]{1,0:T(8,128)}, u32[]{:S(2)}) copy-start(f32[80,256]{1,0:T(8,128)} %param.9) | copy-start | bytes 245764
  15.3 11.6 %copy-start.4 = (s32[256]{0:T(256)S(1)}, s32[256]{0:T(256)}, u32[]{:S(2)}) copy-start(s32[256]{0:T(256)} %param.14) | copy-start | bytes 3076
  15.3 36.0 %all-to-all-start = ((bf16[128,24,256]{2,1,0:T(8,128)(2,1)}), bf16[128,24,256]{2,1,0:T(8,128)(2,1)S(1)}, u32[]{:S(2)}, u32[]{:S(2)}) async-start(bf16[128,24,256]{2,1,0:T(8,128)(2,1)} %bitcast.33), calls=%async_computation | async-start | bytes 3145728 | tf_op jit(solution)/shard_map/all_to_all | solution.py:20
  51.4 3.6 %copy-start.1 = (bf16[128,24,256]{2,1,0:T(8,128)(2,1)}, bf16[128,24,256]{2,1,0:T(8,128)(2,1)S(1)}, u32[]{:S(2)}) copy-start(bf16[128,24,256]{2,1,0:T(8,128)(2,1)S(1)} %all-to-all-done) | copy-start | bytes 4718596
  52.5 2.5 %collective-permute-start = (f32[2,80,256]{2,1,0:T(8,128)S(1)}, f32[2,80,256]{2,1,0:T(8,128)S(1)}, u32[]{:S(2)}, u32[]{:S(2)}) collective-permute-start(f32[2,80,256]{2,1,0:T(8,128)S(1)} %fusion.11), channel_id=1, source_target_pairs={{0,1},{1,0},{2,3},{3,2},{4,5},{5,4},{6,7},{7,6},{8,9},{9,8},{10,11... | collective-permute-start | bytes 491528 | tf_op jit(solution)/shard_map/ppermute | solution.py:279
  80.2 14.5 %all-to-all-start.3 = ((bf16[16,80,256]{2,1,0:T(8,128)(2,1)}), bf16[16,80,256]{2,1,0:T(8,128)(2,1)S(1)}, u32[]{:S(2)}, u32[]{:S(2)}) async-start(bf16[16,80,256]{2,1,0:T(8,128)(2,1)} %broadcast_in_dim.56), calls=%async_computation.3 | async-start | bytes 1310720 | tf_op jit(solution)/shard_map/all_to_all | solution.py:20
  96.4 7.3 %copy-start.3 = (s32[10,1,256]{2,1,0:T(1,128)S(1)}, s32[10,1,256]{2,1,0:T(1,128)}, u32[]{:S(2)}) copy-start(s32[10,1,256]{2,1,0:T(1,128)} %get-tuple-element.9) | copy-start | bytes 30724
  96.4 25.2 %all-to-all-start.4 = ((bf16[8,320,256]{2,1,0:T(8,128)(2,1)}), bf16[8,320,256]{2,1,0:T(8,128)(2,1)}, u32[]{:S(2)}, u32[]{:S(2)}) async-start(bf16[8,320,256]{2,1,0:T(8,128)(2,1)} %bitcast.13), calls=%async_computation.4 | async-start | bytes 2621440 | tf_op jit(solution)/shard_map/all_to_all | solution.py:20

commit v5 on v4

--- a/solution.py
+++ b/solution.py
@@ -62,7 +62,7 @@
         base_ref[...] = jnp.zeros_like(base_ref)
         offs_ref[...] = jnp.zeros_like(offs_ref)
         for i in range(lanes):
-            at_ref[1, 0, i] = rows_out
+            at_ref[1, 0, i] = 2 * rows_out
 
     @pl.when(step > 0)
     def _():
@@ -84,17 +84,17 @@
     rank = jnp.sum(table * (earlier + base_ref[:, :1]), axis=0, keepdims=True)
     base_ref[...] += jnp.sum(table, axis=1, keepdims=True)
     place = pair * per_pair + rank
-    place_ref[0] = jnp.where(live == 0.0, pairs * per_pair, place).astype(jnp.int32)
+    place_ref[0] = (2.0 * jnp.where(live == 0.0, pairs * per_pair, place)).astype(jnp.int32)
     wire = place + (WIRE - half) * quotient(place, half)
-    wire_ref[now] = wire.astype(jnp.int32)
+    wire_ref[now] = (2.0 * wire).astype(jnp.int32)
     handover(now).start()
     row64 = (lax.broadcasted_iota(jnp.int32, (256, lanes), 0) & 63).astype(F32)
     offs_ref[...] += dot((table * off).astype(BF16), onehot(row64 == rank), ((1,), (1,)))
 
     def move(slot, first, last):
         for i in range(first, last):
-            row = pl.ds(at_ref[slot, 0, i], 1)
-            wide_ref[:, row, :] = stage_ref[:, i : i + 1, :]
+            row = pl.ds(pl.multiple_of(at_ref[slot, 0, i], 2), 2)
+            wide_ref[row, :] = stage_ref[2 * i : 2 * i + 2, :]
 
     solved = [
         dot(inv_ref[b], rhs_ref[b * n : (b + 1) * n, :]).astype(BF16) for b in range(GROUP)
@@ -104,10 +104,9 @@
     move(before, lanes // 2, lanes)
     depth = lax.broadcasted_iota(jnp.int32, (k, 2 * 128), 0)
     for b in range(GROUP):
-        own = slice(b * k, (b + 1) * k)
         part = jnp.where(depth < counts_ref[step * GROUP + b], parts[b], 0.0)
-        stage_ref[0, own, :] = part[:, :128]
-        stage_ref[1, own, :] = part[:, 128:]
+        stage_ref[pl.ds(2 * b * k, k, stride=2), :] = part[:, :128]
+        stage_ref[pl.ds(2 * b * k + 1, k, stride=2), :] = part[:, 128:]
 
     @pl.when(step == pl.num_programs(0) - 1)
     def _():
@@ -120,21 +119,29 @@
         groups = pairs // 4
         member = iota((groups, pairs), 0) == quotient(iota((groups, pairs), 1), 4)
         wanted = dot(onehot(member), spread)
-        level = lax.broadcasted_iota(jnp.int32, (WIRE - half, 128), 0)
-        for h in range(2):
-            cut = slice(128 * h, 128 * (h + 1))
-            for v in range(devs):
-                one = jnp.broadcast_to(wanted[2 * v : 2 * v + 1, cut], level.shape)
-                two = jnp.broadcast_to(wanted[2 * v + 1 : 2 * v + 2, cut], level.shape)
-                tail = jnp.where(level == 1, one, jnp.where(level == 2, two, 0.0))
-                for d in range(v, rows_out // WIRE, devs):
-                    own = jnp.broadcast_to(offs_ref[d // 2 : d // 2 + 1, cut], level.shape)
-                    w = d * WIRE + half
-                    wide_ref[h, w : w + WIRE - half, :] = jnp.where(level == 0, own, tail)
+        level = lax.broadcasted_iota(jnp.int32, (2 * (WIRE - half), 128), 0)
+
+        def spread_rows(parts, rest):
+            for at, part in parts:
+                rest = jnp.where(level == at, jnp.broadcast_to(part, level.shape), rest)
+            return rest
+
+        for v in range(devs):
+            rows = [wanted[2 * v + r : 2 * v + r + 1, :] for r in range(2)]
+            fixed = spread_rows(
+                [(2 + 2 * r + h, rows[r][:, 128 * h : 128 * (h + 1)]) for r in range(2) for h in range(2)],
+                jnp.zeros(level.shape, F32),
+            )
+            for d in range(v, rows_out // WIRE, devs):
+                own = [(h, offs_ref[d // 2 : d // 2 + 1, 128 * h : 128 * (h + 1)]) for h in range(2)]
+                w = 2 * (d * WIRE + half)
+                wide_ref[w : w + 2 * (WIRE - half), :] = spread_rows(own, fixed)
         for t in range(rows_out // 256):
             rows = slice(256 * t, 256 * (t + 1))
-            out_ref[rows, :128] = wide_ref[0, rows, :].astype(BF16)
-            out_ref[rows, 128:] = wide_ref[1, rows, :].astype(BF16)
+            for h in range(2):
+                out_ref[rows, 128 * h : 128 * (h + 1)] = wide_ref[
+                    pl.ds(512 * t + h, 256, stride=2), :
+                ].astype(BF16)
 
 
 def middle_kernel(rhs_ref, inv_ref, couple_ref, solved_ref, w_ref):
@@ -158,19 +165,23 @@
     def gather(step, first, last):
         here = place_ref.at[pl.ds(step * lanes, lanes)]
         for i in range(first, last):
-            row = pl.ds(here[i], 1)
-            pick_ref[:, i : i + 1, :] = wide_ref[:, row, :]
+            row = pl.ds(pl.multiple_of(here[i], 2), 2)
+            pick_ref[2 * i : 2 * i + 2, :] = wide_ref[row, :]
 
     @pl.when(step == 0)
     def _():
         for t in range(slots // 256):
             rows = slice(256 * t, 256 * (t + 1))
-            wide_ref[0, rows, :] = back_ref[rows, :128].astype(F32)
-            wide_ref[1, rows, :] = back_ref[rows, 128:].astype(F32)
-        wide_ref[:, slots:, :] = jnp.zeros_like(wide_ref[:, slots:, :])
+            for h in range(2):
+                wide_ref[pl.ds(512 * t + h, 256, stride=2), :] = back_ref[
+                    rows, 128 * h : 128 * (h + 1)
+                ].astype(F32)
+        wide_ref[2 * slots :, :] = jnp.zeros_like(wide_ref[2 * slots :, :])
         gather(step, 0, lanes)
 
-    picked = jnp.concatenate([pick_ref[0], pick_ref[1]], axis=1).astype(BF16)
+    picked = jnp.concatenate(
+        [pick_ref[pl.ds(h, lanes, stride=2), :] for h in range(2)], axis=1
+    ).astype(BF16)
     empty = jnp.zeros((k, picked.shape[1]), BF16)
     for b in range(GROUP):
         rows = slice(b * n, (b + 1) * n)
@@ -232,8 +243,8 @@
                 pl.BlockSpec((1, 1, lanes), lambda i, at: (i, 0, 0)),
             ],
             scratch_shapes=[
-                pltpu.VMEM((2, owners * WIRE + 8, 128), f32),
-                pltpu.VMEM((2, lanes, 128), f32),
+                pltpu.VMEM((2 * (owners * WIRE + 8), 128), f32),
+                pltpu.VMEM((2 * lanes, 128), f32),
                 pltpu.VMEM((pairs, 128), f32),
                 pltpu.VMEM((pairs, 256), f32),
                 pltpu.VMEM((2, 1, lanes), jnp.int32),
@@ -309,14 +320,14 @@
             ],
             out_specs=pl.BlockSpec((GROUP * n, cols), lambda i, at: (i, 0)),
             scratch_shapes=[
-                pltpu.VMEM((2, slots + 8, 128), f32),
-                pltpu.VMEM((2, lanes, 128), f32),
+                pltpu.VMEM((2 * (slots + 8), 128), f32),
+                pltpu.VMEM((2 * lanes, 128), f32),
             ],
         ),
         out_shape=jax.ShapeDtypeStruct((nb * n, cols), bf16),
         cost_estimate=cost(4 * 10**9, 14 * 10**6),
         name="tail",
-    )(jnp.pad(place.reshape(-1), (0, lanes), constant_values=slots), back, solved, weights)
+    )(jnp.pad(place.reshape(-1), (0, lanes), constant_values=2 * slots), back, solved, weights)
     return interior, values.astype(f32)
 
 

time: 134 us -> 134 us (level)
  no operation moved by 1% of the time
where the time goes in v5:
time: 134 us; the launch traced here: 132 us
  waiting for transfers between devices  39.5 us (29%)
  Pallas kernels  36 us (27%)
  starting transfers between devices  23.8 us (18%)
  blocking collectives  23.2 us (17%)
  local copies, waits for them, and re-layouts  5.72 us (4%)
  matrix products  1.83 us (1%)
  other arithmetic  1.49 us (1%)
    all_to_all x3, waiting for transfers between devices, exchange(): return lax.all_to_all(blocks, axis, 0, 0, tiled=True)  38.5 us
    all_to_all x2, blocking collectives, exchange(): return lax.all_to_all(blocks, axis, 0, 0, tiled=True)  23.2 us
    all_to_all x3, starting transfers between devices, exchange(): return lax.all_to_all(blocks, axis, 0, 0, tiled=True)  22.4 us
    pallas_call x1, Pallas kernels, shards(): pl.pallas_call(functools.partial(forward_kernel, (per_pair, half, pair_ro...  14.4 us
    pallas_call x1, Pallas kernels, shards(): pl.pallas_call(tail_kernel, grid_spec=pltpu.PrefetchScalarGridSpec(num_sc...  11 us
    pallas_call x1, Pallas kernels, shards(): pl.pallas_call(middle_kernel, grid=(steps,), in_specs=[*block_specs, pl.B...  10.6 us
  transfers between devices with their start and end apart: 4, of which 4 were waited for; matrix products, arithmetic and copies ran while one was open for 3% of the time, Pallas kernels for 8%

profile of v5, /device:TPU:1, one launch (start us, length us, event | category | flops | bytes accessed | tf_op | source)
XLA Modules:
  0.0 132.4 jit_solution(7341567655000616558)
XLA Ops:
  0.6 0.0 copy-start
  0.6 14.4 %forward.1 = (bf16[3072,256]{1,0:T(8,128)(2,1)}, s32[10,1,256]{2,1,0:T(1,128)}) custom-call(s32[40]{0:T(128)} %counts_ref.1, s32[40,64]{1,0:T(8,128)} %map_ref.1, bf16[10240,256]{1,0:T(8,128)(2,1)} %rhs_ref.3, bf16[40,256,256]{2,1,0:T(8,128)(2,1)} %inv_ref.3, bf16[40,2,64,256]{3,2,1,0:T(8,128)(2,1)} %couple_ref.3), custom_call_target="tpu_custom_call" | custom-call | flops 2000000000 | bytes 14000000 | tf_op jit(solution)/shard_map/forward/pallas_call | solution.py:230
  15.0 0.0 copy-start.2
  15.0 0.0 copy-start.4
  15.1 11.5 %all-to-all-start = ((bf16[128,24,256]{2,1,0:T(8,128)(2,1)}), bf16[128,24,256]{2,1,0:T(8,128)(2,1)S(1)}, u32[]{:S(2)}, u32[]{:S(2)}) async-start(bf16[128,24,256]{2,1,0:T(8,128)(2,1)} %bitcast.33), calls=%async_computation | async-start | bytes 3145728 | tf_op jit(solution)/shard_map/all_to_all | solution.py:20
  26.6 0.0 copy-done.2
  26.6 0.1 copy.21
  26.7 0.0 copy-done.4
  26.7 0.7 gather_fusion
  27.4 0.1 select_bitcast_fusion
  27.5 0.1 copy.22
  27.7 10.6 %middle.1 = (bf16[10240,256]{1,0:T(8,128)(2,1)}, bf16[20,256,128]{2,1,0:T(8,128)(2,1)}) custom-call(bf16[10240,256]{1,0:T(8,128)(2,1)} %rhs_ref.3, bf16[40,256,256]{2,1,0:T(8,128)(2,1)} %inv_ref.3, bf16[40,2,64,256]{3,2,1,0:T(8,128)(2,1)} %couple_ref.3), custom_call_target="tpu_custom_call" | custom-call | flops 2000000000 | bytes 20000000 | tf_op jit(solution)/shard_map/middle/pallas_call | solution.py:263
  38.2 12.9 %all-to-all-done = bf16[128,24,256]{2,1,0:T(8,128)(2,1)S(1)} async-done(((bf16[128,24,256]{2,1,0:T(8,128)(2,1)}), bf16[128,24,256]{2,1,0:T(8,128)(2,1)S(1)}, u32[]{:S(2)}, u32[]{:S(2)}) %all-to-all-start) | async-done | bytes 1572896 | tf_op jit(solution)/shard_map/all_to_all | solution.py:20
  51.1 0.0 copy-start.1
  51.1 0.2 fusion.18
  51.3 0.1 copy.31
  51.4 0.1 copy.30
  51.5 0.1 copy.32
  51.6 0.1 eq.51
  51.7 0.5 fusion.11
  52.2 1.4 %collective-permute-start = (f32[2,80,256]{2,1,0:T(8,128)S(1)}, f32[2,80,256]{2,1,0:T(8,128)S(1)}, u32[]{:S(2)}, u32[]{:S(2)}) collective-permute-start(f32[2,80,256]{2,1,0:T(8,128)S(1)} %fusion.11), channel_id=1, source_target_pairs={{0,1},{1,0},{2,3},{3,2},{4,5},{5,4},{6,7},{7,6},{8,9},{9,8},{10,11... | collective-permute-start | bytes 491528 | tf_op jit(solution)/shard_map/ppermute | solution.py:290
  53.7 1.0 collective-permute-done
  54.7 0.0 copy-done.1
  54.8 9.2 %all_to_all.25 = bf16[4,160,256]{2,1,0:T(8,128)(2,1)S(1)} all-to-all(bf16[4,160,256]{2,1,0:T(8,128)(2,1)S(1)} %broadcast_in_dim.55), channel_id=1, replica_groups=mesh['y'=4,'x'=4,'z'=4,'c'=2] {'z'}, dimensions={0} | all-to-all | bytes 655360 | tf_op jit(solution)/shard_map/all_to_all | solution.py:20
  63.9 0.0 copy-done
  64.0 0.7 fusion.2
  64.7 0.2 copy.26
  64.9 14.0 %all_to_all.26 = bf16[16,80,256]{2,1,0:T(8,128)(2,1)S(1)} all-to-all(bf16[16,80,256]{2,1,0:T(8,128)(2,1)S(1)} %bitcast.30), channel_id=1, replica_groups=mesh['y'=4,'x'=4,'z'=4,'c'=2] {'y','x'}, dimensions={0} | all-to-all | bytes 1310720 | tf_op jit(solution)/shard_map/all_to_all | solution.py:20
  79.0 0.1 reduce_sum.12
  79.1 0.9 broadcast_in_dim.56
  80.0 3.6 %all-to-all-start.3 = ((bf16[16,80,256]{2,1,0:T(8,128)(2,1)}), bf16[16,80,256]{2,1,0:T(8,128)(2,1)S(1)}, u32[]{:S(2)}, u32[]{:S(2)}) async-start(bf16[16,80,256]{2,1,0:T(8,128)(2,1)} %broadcast_in_dim.56), calls=%async_computation.3 | async-start | bytes 1310720 | tf_op jit(solution)/shard_map/all_to_all | solution.py:20
  83.6 1.2 slice.20
  84.8 0.1 reshape.100
  84.9 9.5 %all-to-all-done.3 = bf16[16,80,256]{2,1,0:T(8,128)(2,1)S(1)} async-done(((bf16[16,80,256]{2,1,0:T(8,128)(2,1)}), bf16[16,80,256]{2,1,0:T(8,128)(2,1)S(1)}, u32[]{:S(2)}, u32[]{:S(2)}) %all-to-all-start.3) | async-done | bytes 655392 | tf_op jit(solution)/shard_map/all_to_all | solution.py:20
  94.4 0.6 fusion.8
  95.0 1.1 copy.28
  96.2 0.0 copy-start.3
  96.2 7.3 %all-to-all-start.4 = ((bf16[8,320,256]{2,1,0:T(8,128)(2,1)}), bf16[8,320,256]{2,1,0:T(8,128)(2,1)}, u32[]{:S(2)}, u32[]{:S(2)}) async-start(bf16[8,320,256]{2,1,0:T(8,128)(2,1)} %bitcast.13), calls=%async_computation.4 | async-start | bytes 2621440 | tf_op jit(solution)/shard_map/all_to_all | solution.py:20
  103.5 0.0 copy-done.3
  103.5 0.6 pad.8.place_ref
  104.1 1.2 bitcast_convert_fusion
  105.3 16.1 %all-to-all-done.4 = bf16[8,320,256]{2,1,0:T(8,128)(2,1)} async-done(((bf16[8,320,256]{2,1,0:T(8,128)(2,1)}), bf16[8,320,256]{2,1,0:T(8,128)(2,1)}, u32[]{:S(2)}, u32[]{:S(2)}) %all-to-all-start.4) | async-done | bytes 1310752 | tf_op jit(solution)/shard_map/all_to_all | solution.py:20
  121.4 11.0 %tail.1 = bf16[10240,256]{1,0:T(8,128)(2,1)} custom-call(s32[2816]{0:T(1024)} %pad.8.place_ref, bf16[2560,256]{1,0:T(8,128)(2,1)} %bitcast.14.back_ref, bf16[10240,256]{1,0:T(8,128)(2,1)} %get-tuple-element.14.solved_ref, bf16[20,256,128]{2,1,0:T(8,128)(2,1)} %get-tuple-element.15.w_ref), custom_call_target="tpu_custom_call" | custom-call | flops 4000000000 | bytes 14000000 | tf_op jit(solution)/shard_map/tail/pallas_call | solution.py:311
  (14 shorter events, 0.2 us)
Async XLA Ops:
  0.6 63.3 %copy-start = (bf16[1280,640]{1,0:T(8,128)(2,1)S(1)}, bf16[1280,640]{1,0:T(8,128)(2,1)}, u32[]{:S(2)}) copy-start(bf16[1280,640]{1,0:T(8,128)(2,1)} %param.15) | copy-start | bytes 4915204
  15.0 11.5 %copy-start.2 = (f32[80,256]{1,0:T(8,128)S(1)}, f32[80,256]{1,0:T(8,128)}, u32[]{:S(2)}) copy-start(f32[80,256]{1,0:T(8,128)} %param.9) | copy-start | bytes 245764
  15.0 11.6 %copy-start.4 = (s32[256]{0:T(256)S(1)}, s32[256]{0:T(256)}, u32[]{:S(2)}) copy-start(s32[256]{0:T(256)} %param.14) | copy-start | bytes 3076
  15.1 36.0 %all-to-all-start = ((bf16[128,24,256]{2,1,0:T(8,128)(2,1)}), bf16[128,24,256]{2,1,0:T(8,128)(2,1)S(1)}, u32[]{:S(2)}, u32[]{:S(2)}) async-start(bf16[128,24,256]{2,1,0:T(8,128)(2,1)} %bitcast.33), calls=%async_computation | async-start | bytes 3145728 | tf_op jit(solution)/shard_map/all_to_all | solution.py:20
  51.1 3.6 %copy-start.1 = (bf16[128,24,256]{2,1,0:T(8,128)(2,1)}, bf16[128,24,256]{2,1,0:T(8,128)(2,1)S(1)}, u32[]{:S(2)}) copy-start(bf16[128,24,256]{2,1,0:T(8,128)(2,1)S(1)} %all-to-all-done) | copy-start | bytes 4718596
  52.2 2.5 %collective-permute-start = (f32[2,80,256]{2,1,0:T(8,128)S(1)}, f32[2,80,256]{2,1,0:T(8,128)S(1)}, u32[]{:S(2)}, u32[]{:S(2)}) collective-permute-start(f32[2,80,256]{2,1,0:T(8,128)S(1)} %fusion.11), channel_id=1, source_target_pairs={{0,1},{1,0},{2,3},{3,2},{4,5},{5,4},{6,7},{7,6},{8,9},{9,8},{10,11... | collective-permute-start | bytes 491528 | tf_op jit(solution)/shard_map/ppermute | solution.py:290
  80.0 14.5 %all-to-all-start.3 = ((bf16[16,80,256]{2,1,0:T(8,128)(2,1)}), bf16[16,80,256]{2,1,0:T(8,128)(2,1)S(1)}, u32[]{:S(2)}, u32[]{:S(2)}) async-start(bf16[16,80,256]{2,1,0:T(8,128)(2,1)} %broadcast_in_dim.56), calls=%async_computation.3 | async-start | bytes 1310720 | tf_op jit(solution)/shard_map/all_to_all | solution.py:20
  96.2 7.3 %copy-start.3 = (s32[10,1,256]{2,1,0:T(1,128)S(1)}, s32[10,1,256]{2,1,0:T(1,128)}, u32[]{:S(2)}) copy-start(s32[10,1,256]{2,1,0:T(1,128)} %get-tuple-element.9) | copy-start | bytes 30724
  96.2 25.2 %all-to-all-start.4 = ((bf16[8,320,256]{2,1,0:T(8,128)(2,1)}), bf16[8,320,256]{2,1,0:T(8,128)(2,1)}, u32[]{:S(2)}, u32[]{:S(2)}) async-start(bf16[8,320,256]{2,1,0:T(8,128)(2,1)} %bitcast.13), calls=%async_computation.4 | async-start | bytes 2621440 | tf_op jit(solution)/shard_map/all_to_all | solution.py:20

commit v6 on v5

--- a/solution.py
+++ b/solution.py
@@ -13,6 +13,7 @@
 DEV = ("z", "c")
 WIRE = 24
 GROUP = 4
+CHUNKS = 2
 F32, BF16 = jnp.float32, jnp.bfloat16
 
 
@@ -51,7 +52,6 @@
     k = couple_ref.shape[1]
     lanes = GROUP * k
     rows_out = out_ref.shape[0]
-    now, before = lax.rem(step, 2), lax.rem(step + 1, 2)
 
     def handover(slot):
         return pltpu.make_async_copy(wire_ref.at[slot], at_ref.at[slot], sem.at[slot])
@@ -61,57 +61,63 @@
         stage_ref[...] = jnp.zeros_like(stage_ref)
         base_ref[...] = jnp.zeros_like(base_ref)
         offs_ref[...] = jnp.zeros_like(offs_ref)
-        for i in range(lanes):
-            at_ref[1, 0, i] = 2 * rows_out
-
-    @pl.when(step > 0)
-    def _():
-        handover(before).wait()
-
-    slot = jnp.concatenate(
-        [map_ref[pl.ds(step * GROUP + b, 1), :] for b in range(GROUP)], axis=1
-    ).astype(F32)
-    at = lax.broadcasted_iota(jnp.int32, (1, k), 1)
-    live = jnp.concatenate(
-        [jnp.where(at < counts_ref[step * GROUP + b], 1.0, 0.0) for b in range(GROUP)], axis=1
-    )
-    pair = quotient(slot, pair_rows)
-    off = slot - pair_rows * pair
-    table = jnp.where(iota((pairs, lanes), 0) == pair, 1.0, 0.0)
-    earlier = dot(
-        table.astype(BF16), onehot(iota((lanes, lanes), 0) < iota((lanes, lanes), 1))
-    )
-    rank = jnp.sum(table * (earlier + base_ref[:, :1]), axis=0, keepdims=True)
-    base_ref[...] += jnp.sum(table, axis=1, keepdims=True)
-    place = pair * per_pair + rank
-    place_ref[0] = (2.0 * jnp.where(live == 0.0, pairs * per_pair, place)).astype(jnp.int32)
-    wire = place + (WIRE - half) * quotient(place, half)
-    wire_ref[now] = (2.0 * wire).astype(jnp.int32)
-    handover(now).start()
-    row64 = (lax.broadcasted_iota(jnp.int32, (256, lanes), 0) & 63).astype(F32)
-    offs_ref[...] += dot((table * off).astype(BF16), onehot(row64 == rank), ((1,), (1,)))
+        wire_ref[1] = jnp.full((1, lanes), 2 * rows_out, jnp.int32)
 
     def move(slot, first, last):
         for i in range(first, last):
             row = pl.ds(pl.multiple_of(at_ref[slot, 0, i], 2), 2)
             wide_ref[row, :] = stage_ref[2 * i : 2 * i + 2, :]
 
-    solved = [
-        dot(inv_ref[b], rhs_ref[b * n : (b + 1) * n, :]).astype(BF16) for b in range(GROUP)
-    ]
-    move(before, 0, lanes // 2)
-    parts = [dot(couple_ref[b], solved[b]) for b in range(GROUP)]
-    move(before, lanes // 2, lanes)
-    depth = lax.broadcasted_iota(jnp.int32, (k, 2 * 128), 0)
-    for b in range(GROUP):
-        part = jnp.where(depth < counts_ref[step * GROUP + b], parts[b], 0.0)
-        stage_ref[pl.ds(2 * b * k, k, stride=2), :] = part[:, :128]
-        stage_ref[pl.ds(2 * b * k + 1, k, stride=2), :] = part[:, 128:]
+    for now in range(CHUNKS):
+        before, c0 = 1 - now, now * GROUP
+        first = step * (CHUNKS * GROUP) + c0
+        slot = jnp.concatenate(
+            [map_ref[pl.ds(first + b, 1), :] for b in range(GROUP)], axis=1
+        ).astype(F32)
+        at = lax.broadcasted_iota(jnp.int32, (1, k), 1)
+        live = jnp.concatenate(
+            [jnp.where(at < counts_ref[first + b], 1.0, 0.0) for b in range(GROUP)], axis=1
+        )
+        pair = quotient(slot, pair_rows)
+        off = slot - pair_rows * pair
+        table = jnp.where(iota((pairs, lanes), 0) == pair, 1.0, 0.0)
+        earlier = dot(
+            table.astype(BF16), onehot(iota((lanes, lanes), 0) < iota((lanes, lanes), 1))
+        )
+        rank = jnp.sum(table * (earlier + base_ref[:, :1]), axis=0, keepdims=True)
+        base_ref[...] += jnp.sum(table, axis=1, keepdims=True)
+        place = pair * per_pair + rank
+        place_ref[now] = (2.0 * jnp.where(live == 0.0, pairs * per_pair, place)).astype(jnp.int32)
+        wire = place + (WIRE - half) * quotient(place, half)
+        wire_ref[now] = (2.0 * wire).astype(jnp.int32)
+        row64 = (lax.broadcasted_iota(jnp.int32, (256, lanes), 0) & 63).astype(F32)
+        offs_ref[...] += dot((table * off).astype(BF16), onehot(row64 == rank), ((1,), (1,)))
+
+        if now == 0:
+
+            @pl.when(step == 0)
+            def _():
+                handover(1).start()
+
+        solved = [
+            dot(inv_ref[b], rhs_ref[b * n : (b + 1) * n, :]).astype(BF16)
+            for b in range(c0, c0 + GROUP)
+        ]
+        handover(before).wait()
+        handover(now).start()
+        move(before, 0, lanes // 2)
+        parts = [dot(couple_ref[c0 + b], solved[b]) for b in range(GROUP)]
+        move(before, lanes // 2, lanes)
+        depth = lax.broadcasted_iota(jnp.int32, (k, 2 * 128), 0)
+        for b in range(GROUP):
+            part = jnp.where(depth < counts_ref[first + b], parts[b], 0.0)
+            stage_ref[pl.ds(2 * b * k, k, stride=2), :] = part[:, :128]
+            stage_ref[pl.ds(2 * b * k + 1, k, stride=2), :] = part[:, 128:]
 
     @pl.when(step == pl.num_programs(0) - 1)
     def _():
-        handover(now).wait()
-        move(now, 0, lanes)
+        handover(1).wait()
+        move(1, 0, lanes)
         offs = offs_ref[...]
         p = lax.broadcasted_iota(jnp.int32, offs.shape, 0)
         lane = lax.broadcasted_iota(jnp.int32, offs.shape, 1)
@@ -158,8 +164,9 @@
 def tail_kernel(place_ref, back_ref, solved_ref, w_ref, out_ref, wide_ref, pick_ref):
     n = w_ref.shape[1]
     k = w_ref.shape[2] // 2
+    group = 2 * w_ref.shape[0]
     slots = back_ref.shape[0]
-    lanes = GROUP * k
+    lanes = group * k
     step = pl.program_id(0)
 
     def gather(step, first, last):
@@ -183,7 +190,7 @@
         [pick_ref[pl.ds(h, lanes, stride=2), :] for h in range(2)], axis=1
     ).astype(BF16)
     empty = jnp.zeros((k, picked.shape[1]), BF16)
-    for b in range(GROUP):
+    for b in range(group):
         rows = slice(b * n, (b + 1) * n)
         own = picked[b * k : (b + 1) * k, :]
         pad = [own, empty] if b % 2 == 0 else [empty, own]
@@ -227,20 +234,21 @@
         pl.BlockSpec((GROUP * n, cols), lambda i: (i, 0)),
         pl.BlockSpec((GROUP, n, n), lambda i: (i, 0, 0)),
     ]
+    wide = CHUNKS * GROUP
     sent, place = pl.pallas_call(
         functools.partial(forward_kernel, (per_pair, half, pair_rows, pairs, devs)),
         grid_spec=pltpu.PrefetchScalarGridSpec(
             num_scalar_prefetch=1,
-            grid=(steps,),
+            grid=(steps // CHUNKS,),
             in_specs=[
                 pl.BlockSpec((nb, k), lambda i, at: (0, 0)),
-                pl.BlockSpec((GROUP * n, cols), lambda i, at: (i, 0)),
-                pl.BlockSpec((GROUP, n, n), lambda i, at: (i, 0, 0)),
-                pl.BlockSpec((GROUP, None, k, n), lambda i, at: (i, 0, 0, 0)),
+                pl.BlockSpec((wide * n, cols), lambda i, at: (i, 0)),
+                pl.BlockSpec((wide, n, n), lambda i, at: (i, 0, 0)),
+                pl.BlockSpec((wide, None, k, n), lambda i, at: (i, 0, 0, 0)),
             ],
             out_specs=[
                 pl.BlockSpec((owners * WIRE, cols), lambda i, at: (0, 0)),
-                pl.BlockSpec((1, 1, lanes), lambda i, at: (i, 0, 0)),
+                pl.BlockSpec((CHUNKS, 1, lanes), lambda i, at: (i, 0, 0)),
             ],
             scratch_shapes=[
                 pltpu.VMEM((2 * (owners * WIRE + 8), 128), f32),
@@ -312,22 +320,22 @@
         tail_kernel,
         grid_spec=pltpu.PrefetchScalarGridSpec(
             num_scalar_prefetch=1,
-            grid=(steps,),
+            grid=(steps // CHUNKS,),
             in_specs=[
                 pl.BlockSpec((slots, cols), lambda i, at: (0, 0)),
-                pl.BlockSpec((GROUP * n, cols), lambda i, at: (i, 0)),
-                pl.BlockSpec((GROUP // 2, n, 2 * k), lambda i, at: (i, 0, 0)),
-            ],
-            out_specs=pl.BlockSpec((GROUP * n, cols), lambda i, at: (i, 0)),
+                pl.BlockSpec((wide * n, cols), lambda i, at: (i, 0)),
+                pl.BlockSpec((wide // 2, n, 2 * k), lambda i, at: (i, 0, 0)),
+            ],
+            out_specs=pl.BlockSpec((wide * n, cols), lambda i, at: (i, 0)),
             scratch_shapes=[
                 pltpu.VMEM((2 * (slots + 8), 128), f32),
-                pltpu.VMEM((2 * lanes, 128), f32),
+                pltpu.VMEM((2 * wide * k, 128), f32),
             ],
         ),
         out_shape=jax.ShapeDtypeStruct((nb * n, cols), bf16),
         cost_estimate=cost(4 * 10**9, 14 * 10**6),
         name="tail",
-    )(jnp.pad(place.reshape(-1), (0, lanes), constant_values=2 * slots), back, solved, weights)
+    )(jnp.pad(place.reshape(-1), (0, wide * k), constant_values=2 * slots), back, solved, weights)
     return interior, values.astype(f32)
 
 

time: 134 us -> 130 us (0.970)
  Pallas kernels: 36 us -> 32.8 us
    pallas_call x1, Pallas kernels: 14.4 us -> 12.6 us  [shards(): pl.pallas_call(functools.partial(forward_kernel, (per_pair, half, pair_ro...]
    pallas_call x1, Pallas kernels: 11 us -> 9.59 us  [shards(): pl.pallas_call(tail_kernel, grid_spec=pltpu.PrefetchScalarGridSpec(num_sc...]
where the time goes in v6:
time: 130 us; the launch traced here: 129 us
  waiting for transfers between devices  39.5 us (30%)
  Pallas kernels  32.8 us (25%)
  starting transfers between devices  23.8 us (18%)
  blocking collectives  23.2 us (18%)
  local copies, waits for them, and re-layouts  5.72 us (4%)
  matrix products  1.83 us (1%)
  other arithmetic  1.49 us (1%)
    all_to_all x3, waiting for transfers between devices, exchange(): return lax.all_to_all(blocks, axis, 0, 0, tiled=True)  38.5 us
    all_to_all x2, blocking collectives, exchange(): return lax.all_to_all(blocks, axis, 0, 0, tiled=True)  23.2 us
    all_to_all x3, starting transfers between devices, exchange(): return lax.all_to_all(blocks, axis, 0, 0, tiled=True)  22.4 us
    pallas_call x1, Pallas kernels, shards(): pl.pallas_call(functools.partial(forward_kernel, (per_pair, half, pair_ro...  12.6 us
    pallas_call x1, Pallas kernels, shards(): pl.pallas_call(middle_kernel, grid=(steps,), in_specs=[*block_specs, pl.B...  10.6 us
    pallas_call x1, Pallas kernels, shards(): pl.pallas_call(tail_kernel, grid_spec=pltpu.PrefetchScalarGridSpec(num_sc...  9.59 us
  transfers between devices with their start and end apart: 4, of which 4 were waited for; matrix products, arithmetic and copies ran while one was open for 3% of the time, Pallas kernels for 8%

profile of v6, /device:TPU:1, one launch (start us, length us, event | category | flops | bytes accessed | tf_op | source)
XLA Modules:
  0.0 129.2 jit_solution(15389629818517428702)
XLA Ops:
  0.6 0.0 copy-start
  0.6 12.6 %forward.1 = (bf16[3072,256]{1,0:T(8,128)(2,1)}, s32[10,1,256]{2,1,0:T(1,128)}) custom-call(s32[40]{0:T(128)} %counts_ref.1, s32[40,64]{1,0:T(8,128)} %map_ref.1, bf16[10240,256]{1,0:T(8,128)(2,1)} %rhs_ref.3, bf16[40,256,256]{2,1,0:T(8,128)(2,1)} %inv_ref.3, bf16[40,2,64,256]{3,2,1,0:T(8,128)(2,1)} %couple_ref.3), custom_call_target="tpu_custom_call" | custom-call | flops 2000000000 | bytes 14000000 | tf_op jit(solution)/shard_map/forward/pallas_call | solution.py:238
  13.3 0.0 copy-start.2
  13.3 0.0 copy-start.4
  13.3 11.5 %all-to-all-start = ((bf16[128,24,256]{2,1,0:T(8,128)(2,1)}), bf16[128,24,256]{2,1,0:T(8,128)(2,1)S(1)}, u32[]{:S(2)}, u32[]{:S(2)}) async-start(bf16[128,24,256]{2,1,0:T(8,128)(2,1)} %bitcast.33), calls=%async_computation | async-start | bytes 3145728 | tf_op jit(solution)/shard_map/all_to_all | solution.py:21
  24.8 0.0 copy-done.2
  24.8 0.1 copy.21
  24.9 0.0 copy-done.4
  24.9 0.7 gather_fusion
  25.7 0.1 select_bitcast_fusion
  25.8 0.1 copy.22
  25.9 10.6 %middle.1 = (bf16[10240,256]{1,0:T(8,128)(2,1)}, bf16[20,256,128]{2,1,0:T(8,128)(2,1)}) custom-call(bf16[10240,256]{1,0:T(8,128)(2,1)} %rhs_ref.3, bf16[40,256,256]{2,1,0:T(8,128)(2,1)} %inv_ref.3, bf16[40,2,64,256]{3,2,1,0:T(8,128)(2,1)} %couple_ref.3), custom_call_target="tpu_custom_call" | custom-call | flops 2000000000 | bytes 20000000 | tf_op jit(solution)/shard_map/middle/pallas_call | solution.py:271
  36.5 12.9 %all-to-all-done = bf16[128,24,256]{2,1,0:T(8,128)(2,1)S(1)} async-done(((bf16[128,24,256]{2,1,0:T(8,128)(2,1)}), bf16[128,24,256]{2,1,0:T(8,128)(2,1)S(1)}, u32[]{:S(2)}, u32[]{:S(2)}) %all-to-all-start) | async-done | bytes 1572896 | tf_op jit(solution)/shard_map/all_to_all | solution.py:21
  49.3 0.0 copy-start.1
  49.3 0.2 fusion.18
  49.5 0.1 copy.31
  49.6 0.1 copy.30
  49.7 0.1 copy.32
  49.9 0.1 eq.51
  50.0 0.5 fusion.11
  50.4 1.4 %collective-permute-start = (f32[2,80,256]{2,1,0:T(8,128)S(1)}, f32[2,80,256]{2,1,0:T(8,128)S(1)}, u32[]{:S(2)}, u32[]{:S(2)}) collective-permute-start(f32[2,80,256]{2,1,0:T(8,128)S(1)} %fusion.11), channel_id=1, source_target_pairs={{0,1},{1,0},{2,3},{3,2},{4,5},{5,4},{6,7},{7,6},{8,9},{9,8},{10,11... | collective-permute-start | bytes 491528 | tf_op jit(solution)/shard_map/ppermute | solution.py:298
  51.9 1.0 collective-permute-done
  52.9 0.0 copy-done.1
  53.0 9.2 %all_to_all.25 = bf16[4,160,256]{2,1,0:T(8,128)(2,1)S(1)} all-to-all(bf16[4,160,256]{2,1,0:T(8,128)(2,1)S(1)} %broadcast_in_dim.55), channel_id=1, replica_groups=mesh['y'=4,'x'=4,'z'=4,'c'=2] {'z'}, dimensions={0} | all-to-all | bytes 655360 | tf_op jit(solution)/shard_map/all_to_all | solution.py:21
  62.2 0.0 copy-done
  62.2 0.7 fusion.2
  62.9 0.2 copy.26
  63.2 14.0 %all_to_all.26 = bf16[16,80,256]{2,1,0:T(8,128)(2,1)S(1)} all-to-all(bf16[16,80,256]{2,1,0:T(8,128)(2,1)S(1)} %bitcast.30), channel_id=1, replica_groups=mesh['y'=4,'x'=4,'z'=4,'c'=2] {'y','x'}, dimensions={0} | all-to-all | bytes 1310720 | tf_op jit(solution)/shard_map/all_to_all | solution.py:21
  77.2 0.1 reduce_sum.12
  77.3 0.9 broadcast_in_dim.56
  78.2 3.6 %all-to-all-start.3 = ((bf16[16,80,256]{2,1,0:T(8,128)(2,1)}), bf16[16,80,256]{2,1,0:T(8,128)(2,1)S(1)}, u32[]{:S(2)}, u32[]{:S(2)}) async-start(bf16[16,80,256]{2,1,0:T(8,128)(2,1)} %broadcast_in_dim.56), calls=%async_computation.3 | async-start | bytes 1310720 | tf_op jit(solution)/shard_map/all_to_all | solution.py:21
  81.8 1.2 slice.20
  83.0 0.1 reshape.100
  83.1 9.5 %all-to-all-done.3 = bf16[16,80,256]{2,1,0:T(8,128)(2,1)S(1)} async-done(((bf16[16,80,256]{2,1,0:T(8,128)(2,1)}), bf16[16,80,256]{2,1,0:T(8,128)(2,1)S(1)}, u32[]{:S(2)}, u32[]{:S(2)}) %all-to-all-start.3) | async-done | bytes 655392 | tf_op jit(solution)/shard_map/all_to_all | solution.py:21
  92.6 0.6 fusion.8
  93.3 1.1 copy.28
  94.4 0.0 copy-start.3
  94.4 7.3 %all-to-all-start.4 = ((bf16[8,320,256]{2,1,0:T(8,128)(2,1)}), bf16[8,320,256]{2,1,0:T(8,128)(2,1)}, u32[]{:S(2)}, u32[]{:S(2)}) async-start(bf16[8,320,256]{2,1,0:T(8,128)(2,1)} %bitcast.13), calls=%async_computation.4 | async-start | bytes 2621440 | tf_op jit(solution)/shard_map/all_to_all | solution.py:21
  101.7 0.0 copy-done.3
  101.8 0.6 pad.8.place_ref
  102.4 1.2 bitcast_convert_fusion
  103.6 16.1 %all-to-all-done.4 = bf16[8,320,256]{2,1,0:T(8,128)(2,1)} async-done(((bf16[8,320,256]{2,1,0:T(8,128)(2,1)}), bf16[8,320,256]{2,1,0:T(8,128)(2,1)}, u32[]{:S(2)}, u32[]{:S(2)}) %all-to-all-start.4) | async-done | bytes 1310752 | tf_op jit(solution)/shard_map/all_to_all | solution.py:21
  119.6 9.6 %tail.1 = bf16[10240,256]{1,0:T(8,128)(2,1)} custom-call(s32[3072]{0:T(1024)} %pad.8.place_ref, bf16[2560,256]{1,0:T(8,128)(2,1)} %bitcast.14.back_ref, bf16[10240,256]{1,0:T(8,128)(2,1)} %get-tuple-element.14.solved_ref, bf16[20,256,128]{2,1,0:T(8,128)(2,1)} %get-tuple-element.15.w_ref), custom_call_target="tpu_custom_call" | custom-call | flops 4000000000 | bytes 14000000 | tf_op jit(solution)/shard_map/tail/pallas_call | solution.py:319
  (14 shorter events, 0.2 us)
Async XLA Ops:
  0.6 61.5 %copy-start = (bf16[1280,640]{1,0:T(8,128)(2,1)S(1)}, bf16[1280,640]{1,0:T(8,128)(2,1)}, u32[]{:S(2)}) copy-start(bf16[1280,640]{1,0:T(8,128)(2,1)} %param.15) | copy-start | bytes 4915204
  13.3 11.5 %copy-start.2 = (f32[80,256]{1,0:T(8,128)S(1)}, f32[80,256]{1,0:T(8,128)}, u32[]{:S(2)}) copy-start(f32[80,256]{1,0:T(8,128)} %param.9) | copy-start | bytes 245764
  13.3 11.6 %copy-start.4 = (s32[256]{0:T(256)S(1)}, s32[256]{0:T(256)}, u32[]{:S(2)}) copy-start(s32[256]{0:T(256)} %param.14) | copy-start | bytes 3076
  13.3 36.0 %all-to-all-start = ((bf16[128,24,256]{2,1,0:T(8,128)(2,1)}), bf16[128,24,256]{2,1,0:T(8,128)(2,1)S(1)}, u32[]{:S(2)}, u32[]{:S(2)}) async-start(bf16[128,24,256]{2,1,0:T(8,128)(2,1)} %bitcast.33), calls=%async_computation | async-start | bytes 3145728 | tf_op jit(solution)/shard_map/all_to_all | solution.py:21
  49.3 3.6 %copy-start.1 = (bf16[128,24,256]{2,1,0:T(8,128)(2,1)}, bf16[128,24,256]{2,1,0:T(8,128)(2,1)S(1)}, u32[]{:S(2)}) copy-start(bf16[128,24,256]{2,1,0:T(8,128)(2,1)S(1)} %all-to-all-done) | copy-start | bytes 4718596
  50.4 2.5 %collective-permute-start = (f32[2,80,256]{2,1,0:T(8,128)S(1)}, f32[2,80,256]{2,1,0:T(8,128)S(1)}, u32[]{:S(2)}, u32[]{:S(2)}) collective-permute-start(f32[2,80,256]{2,1,0:T(8,128)S(1)} %fusion.11), channel_id=1, source_target_pairs={{0,1},{1,0},{2,3},{3,2},{4,5},{5,4},{6,7},{7,6},{8,9},{9,8},{10,11... | collective-permute-start | bytes 491528 | tf_op jit(solution)/shard_map/ppermute | solution.py:298
  78.2 14.5 %all-to-all-start.3 = ((bf16[16,80,256]{2,1,0:T(8,128)(2,1)}), bf16[16,80,256]{2,1,0:T(8,128)(2,1)S(1)}, u32[]{:S(2)}, u32[]{:S(2)}) async-start(bf16[16,80,256]{2,1,0:T(8,128)(2,1)} %broadcast_in_dim.56), calls=%async_computation.3 | async-start | bytes 1310720 | tf_op jit(solution)/shard_map/all_to_all | solution.py:21
  94.4 7.3 %copy-start.3 = (s32[10,1,256]{2,1,0:T(1,128)S(1)}, s32[10,1,256]{2,1,0:T(1,128)}, u32[]{:S(2)}) copy-start(s32[10,1,256]{2,1,0:T(1,128)} %get-tuple-element.9) | copy-start | bytes 30724
  94.4 25.2 %all-to-all-start.4 = ((bf16[8,320,256]{2,1,0:T(8,128)(2,1)}), bf16[8,320,256]{2,1,0:T(8,128)(2,1)}, u32[]{:S(2)}, u32[]{:S(2)}) async-start(bf16[8,320,256]{2,1,0:T(8,128)(2,1)} %bitcast.13), calls=%async_computation.4 | async-start | bytes 2621440 | tf_op jit(solution)/shard_map/all_to_all | solution.py:21

commit v7 on v6

--- a/solution.py
+++ b/solution.py
@@ -99,14 +99,15 @@
             def _():
                 handover(1).start()
 
-        solved = [
-            dot(inv_ref[b], rhs_ref[b * n : (b + 1) * n, :]).astype(BF16)
-            for b in range(c0, c0 + GROUP)
+        folded = [
+            dot(couple_ref[b], inv_ref[b]).astype(BF16) for b in range(c0, c0 + GROUP)
         ]
         handover(before).wait()
         handover(now).start()
         move(before, 0, lanes // 2)
-        parts = [dot(couple_ref[c0 + b], solved[b]) for b in range(GROUP)]
+        parts = [
+            dot(folded[b], rhs_ref[(c0 + b) * n : (c0 + b + 1) * n, :]) for b in range(GROUP)
+        ]
         move(before, lanes // 2, lanes)
         depth = lax.broadcasted_iota(jnp.int32, (k, 2 * 128), 0)
         for b in range(GROUP):
@@ -197,6 +198,20 @@
         term = dot(w_ref[b // 2], jnp.concatenate(pad, axis=0))
         gather(step + 1, b * k, (b + 1) * k)
         out_ref[rows, :] = (solved_ref[rows, :].astype(F32) - term).astype(BF16)
+
+
+def serve_kernel(asked_ref, values_ref, returned_ref, out_ref):
+    peers, rows = returned_ref.shape[:2]
+    count = asked_ref.shape[0] // peers
+    per_pair = rows // peers
+    depth = values_ref.shape[0] // peers
+    out_ref[...] = values_ref[...].astype(F32)
+    for j in range(peers):
+        picker = asked_ref[j * count : (j + 1) * count, :] == iota((count, depth), 1)
+        chosen = dot(onehot(picker), values_ref[j * depth : (j + 1) * depth, :])
+        for v in range(peers):
+            part = chosen[v * per_pair : (v + 1) * per_pair, :]
+            returned_ref[v, j * per_pair : (j + 1) * per_pair, :] = part.astype(BF16)
 
 
 def cost(flops, size):
@@ -286,7 +301,8 @@
 
     core = lax.axis_index("c")
     offs = jnp.where(core == 0, got[:, half, :half], got[:, half, half : 2 * half])
-    offs, solved, weights = lax.optimization_barrier((offs, solved, weights))
+    place = jnp.pad(place.reshape(-1), (0, wide * k), constant_values=2 * slots)
+    offs, solved, weights, place = lax.optimization_barrier((offs, solved, weights, place))
     target = jnp.pad(offs, ((0, 0), (0, WIRE - half)), constant_values=-1.0).reshape(1, -1)
     selector = jnp.arange(pair_rows, dtype=jnp.int32)[:, None].astype(bf16) == target
     arrived = jnp.dot(
@@ -307,14 +323,21 @@
     s = lax.axis_index(SEC)
     asked = lax.dynamic_slice_in_dim(got[:, half + 1 : half + 3], s * devs, devs, axis=0)
     asked = asked.reshape(devs, band // pair_rows, 64)[:, :, :per_pair]
-    picker = asked[:, :, :, None] == jnp.arange(pair_rows, dtype=jnp.int32).astype(bf16)
-    returned = jnp.einsum(
-        "vjkr,jrn->vjkn",
-        picker.astype(bf16),
-        values.reshape(-1, pair_rows, cols),
-        preferred_element_type=f32,
-    ).astype(bf16)
-    back = exchange(returned.reshape(devs, -1, cols), DEV).reshape(slots, cols)
+    asked = jnp.swapaxes(asked, 0, 1).astype(f32).reshape(slots, 1)
+    whole = pl.BlockSpec(memory_space=pltpu.VMEM)
+    returned, answer = pl.pallas_call(
+        serve_kernel,
+        in_specs=[whole, whole],
+        out_specs=[whole, whole],
+        out_shape=[
+            jax.ShapeDtypeStruct((devs, slots // devs, cols), bf16),
+            jax.ShapeDtypeStruct((band, cols), f32),
+        ],
+        compiler_params=pltpu.CompilerParams(vmem_limit_bytes=16 << 20),
+        cost_estimate=cost(2 * 10**8, 4 * 10**6),
+        name="serve",
+    )(asked, values)
+    back = exchange(returned, DEV).reshape(slots, cols)
 
     interior = pl.pallas_call(
         tail_kernel,
@@ -335,8 +358,8 @@
         out_shape=jax.ShapeDtypeStruct((nb * n, cols), bf16),
         cost_estimate=cost(4 * 10**9, 14 * 10**6),
         name="tail",
-    )(jnp.pad(place.reshape(-1), (0, wide * k), constant_values=2 * slots), back, solved, weights)
-    return interior, values.astype(f32)
+    )(place, back, solved, weights)
+    return interior, answer
 
 
 def solution(mesh):

time: 130 us -> 130 us (level)
  blocking collectives: 23.2 us -> 47.1 us
  waiting for transfers between devices: 39.5 us -> 22.4 us
  starting transfers between devices: 23.8 us -> 17.2 us
  Pallas kernels: 32.8 us -> 34.8 us
    all_to_all x2 -> x3, blocking collectives: 23.2 us -> 47.1 us  [exchange(): return lax.all_to_all(blocks, axis, 0, 0, tiled=True)]
    all_to_all x3 -> x2, waiting for transfers between devices: 38.5 us -> 21.4 us  [exchange(): return lax.all_to_all(blocks, axis, 0, 0, tiled=True)]
    all_to_all x3 -> x2, starting transfers between devices: 22.4 us -> 15.7 us  [exchange(): return lax.all_to_all(blocks, axis, 0, 0, tiled=True)]
    pallas_call x0 -> x1, Pallas kernels: none -> 2.73 us  [shards(): pl.pallas_call(serve_kernel, in_specs=[whole, whole], out_specs=[whole, w...]
  transfers between devices with their start and end apart: 4 -> 3, of which waited for: 4 -> 3; matrix products, arithmetic and copies ran while one was open for 3% -> 3% of each run, Pallas kernels for 8% -> 8%
where the time goes in v7:
time: 130 us; the launch traced here: 129 us
  blocking collectives  47.1 us (36%)
  Pallas kernels  34.8 us (27%)
  waiting for transfers between devices  22.4 us (17%)
  starting transfers between devices  17.2 us (13%)
  local copies, waits for them, and re-layouts  4.98 us (4%)
    all_to_all x3, blocking collectives, exchange(): return lax.all_to_all(blocks, axis, 0, 0, tiled=True)  47.1 us
    all_to_all x2, waiting for transfers between devices, exchange(): return lax.all_to_all(blocks, axis, 0, 0, tiled=True)  21.4 us
    all_to_all x2, starting transfers between devices, exchange(): return lax.all_to_all(blocks, axis, 0, 0, tiled=True)  15.7 us
    pallas_call x1, Pallas kernels, shards(): pl.pallas_call(functools.partial(forward_kernel, (per_pair, half, pair_ro...  11.9 us
    pallas_call x1, Pallas kernels, shards(): pl.pallas_call(middle_kernel, grid=(steps,), in_specs=[*block_specs, pl.B...  10.6 us
    pallas_call x1, Pallas kernels, shards(): pl.pallas_call(tail_kernel, grid_spec=pltpu.PrefetchScalarGridSpec(num_sc...  9.59 us
    pallas_call x1, Pallas kernels, shards(): pl.pallas_call(serve_kernel, in_specs=[whole, whole], out_specs=[whole, w...  2.73 us
  transfers between devices with their start and end apart: 3, of which 3 were waited for; matrix products, arithmetic and copies ran while one was open for 3% of the time, Pallas kernels for 8%

profile of v7, /device:TPU:1, one launch (start us, length us, event | category | flops | bytes accessed | tf_op | source)
XLA Modules:
  0.0 128.8 jit_solution(9137389365270505093)
XLA Ops:
  0.6 0.0 copy-start
  0.6 11.9 %forward.1 = (bf16[3072,256]{1,0:T(8,128)(2,1)}, s32[10,1,256]{2,1,0:T(1,128)}) custom-call(s32[40]{0:T(128)} %counts_ref.1, s32[40,64]{1,0:T(8,128)} %map_ref.1, bf16[10240,256]{1,0:T(8,128)(2,1)} %rhs_ref.3, bf16[40,256,256]{2,1,0:T(8,128)(2,1)} %inv_ref.3, bf16[40,2,64,256]{3,2,1,0:T(8,128)(2,1)} %couple_ref.3), custom_call_target="tpu_custom_call" | custom-call | flops 2000000000 | bytes 14000000 | tf_op jit(solution)/shard_map/forward/pallas_call | solution.py:253
  12.5 0.0 copy-start.2
  12.6 0.0 copy-start.4
  12.6 0.0 copy-start.3
  12.6 11.5 %all-to-all-start = ((bf16[128,24,256]{2,1,0:T(8,128)(2,1)}), bf16[128,24,256]{2,1,0:T(8,128)(2,1)S(1)}, u32[]{:S(2)}, u32[]{:S(2)}) async-start(bf16[128,24,256]{2,1,0:T(8,128)(2,1)} %bitcast.22), calls=%async_computation | async-start | bytes 3145728 | tf_op jit(solution)/shard_map/all_to_all | solution.py:21
  24.1 0.0 copy-done.2
  24.1 0.1 copy.24
  24.2 0.0 copy-done.4
  24.2 0.7 gather_fusion
  25.0 0.1 select_bitcast_fusion
  25.1 0.1 copy.25
  25.2 0.0 copy-done.3
  25.2 0.6 pad.8.place_ref
  25.8 10.6 %middle.1 = (bf16[10240,256]{1,0:T(8,128)(2,1)}, bf16[20,256,128]{2,1,0:T(8,128)(2,1)}) custom-call(bf16[10240,256]{1,0:T(8,128)(2,1)} %rhs_ref.3, bf16[40,256,256]{2,1,0:T(8,128)(2,1)} %inv_ref.3, bf16[40,2,64,256]{3,2,1,0:T(8,128)(2,1)} %couple_ref.3), custom_call_target="tpu_custom_call" | custom-call | flops 2000000000 | bytes 20000000 | tf_op jit(solution)/shard_map/middle/pallas_call | solution.py:286
  36.4 12.2 %all-to-all-done = bf16[128,24,256]{2,1,0:T(8,128)(2,1)S(1)} async-done(((bf16[128,24,256]{2,1,0:T(8,128)(2,1)}), bf16[128,24,256]{2,1,0:T(8,128)(2,1)S(1)}, u32[]{:S(2)}, u32[]{:S(2)}) %all-to-all-start) | async-done | bytes 1572896 | tf_op jit(solution)/shard_map/all_to_all | solution.py:21
  48.6 0.0 copy-start.1
  48.6 0.2 fusion.8
  48.8 0.1 copy.30
  48.9 0.1 copy.29
  49.0 0.1 copy.31
  49.2 0.1 eq.38
  49.3 0.5 fusion.3
  49.7 1.4 %collective-permute-start = (f32[2,80,256]{2,1,0:T(8,128)S(1)}, f32[2,80,256]{2,1,0:T(8,128)S(1)}, u32[]{:S(2)}, u32[]{:S(2)}) collective-permute-start(f32[2,80,256]{2,1,0:T(8,128)S(1)} %fusion.3), channel_id=1, source_target_pairs={{0,1},{1,0},{2,3},{3,2},{4,5},{5,4},{6,7},{7,6},{8,9},{9,8},{10,11... | collective-permute-start | bytes 491528 | tf_op jit(solution)/shard_map/ppermute | solution.py:314
  51.2 1.0 collective-permute-done
  52.2 0.0 copy-done.1
  52.3 9.2 %all_to_all.25 = bf16[4,160,256]{2,1,0:T(8,128)(2,1)S(1)} all-to-all(bf16[4,160,256]{2,1,0:T(8,128)(2,1)S(1)} %broadcast_in_dim.53), channel_id=1, replica_groups=mesh['y'=4,'x'=4,'z'=4,'c'=2] {'z'}, dimensions={0} | all-to-all | bytes 655360 | tf_op jit(solution)/shard_map/all_to_all | solution.py:21
  61.5 0.0 copy-done
  61.5 0.7 fusion
  62.2 0.2 copy.27
  62.4 14.0 %all_to_all.26 = bf16[16,80,256]{2,1,0:T(8,128)(2,1)S(1)} all-to-all(bf16[16,80,256]{2,1,0:T(8,128)(2,1)S(1)} %bitcast.20), channel_id=1, replica_groups=mesh['y'=4,'x'=4,'z'=4,'c'=2] {'y','x'}, dimensions={0} | all-to-all | bytes 1310720 | tf_op jit(solution)/shard_map/all_to_all | solution.py:21
  76.5 0.1 reduce_sum.12
  76.5 0.9 broadcast_in_dim.54
  77.4 4.3 %all-to-all-start.3 = ((bf16[16,80,256]{2,1,0:T(8,128)(2,1)}), bf16[16,80,256]{2,1,0:T(8,128)(2,1)}, u32[]{:S(2)}, u32[]{:S(2)}) async-start(bf16[16,80,256]{2,1,0:T(8,128)(2,1)} %broadcast_in_dim.54), calls=%async_computation.3 | async-start | bytes 1310720 | tf_op jit(solution)/shard_map/all_to_all | solution.py:21
  81.7 1.2 slice.20
  82.9 0.1 reshape.94
  83.0 0.4 reshape.115.asked_ref
  83.4 9.2 %all-to-all-done.3 = bf16[16,80,256]{2,1,0:T(8,128)(2,1)} async-done(((bf16[16,80,256]{2,1,0:T(8,128)(2,1)}), bf16[16,80,256]{2,1,0:T(8,128)(2,1)}, u32[]{:S(2)}, u32[]{:S(2)}) %all-to-all-start.3) | async-done | bytes 655392 | tf_op jit(solution)/shard_map/all_to_all | solution.py:21
  92.6 2.7 %serve.1 = (bf16[8,320,256]{2,1,0:T(8,128)(2,1)S(1)}, f32[1280,256]{1,0:T(8,128)}) custom-call(f32[2560,1]{1,0:T(8,128)S(1)} %reshape.115.asked_ref, bf16[1280,256]{1,0:T(8,128)(2,1)} %bitcast.10.values_ref), custom_call_target="tpu_custom_call" | custom-call | flops 200000000 | bytes 4000000 | tf_op jit(solution)/shard_map/serve/pallas_call | solution.py:328
  95.3 23.9 %all_to_all.27 = bf16[8,320,256]{2,1,0:T(8,128)(2,1)} all-to-all(bf16[8,320,256]{2,1,0:T(8,128)(2,1)S(1)} %get-tuple-element.18), channel_id=1, replica_groups=mesh['y'=4,'x'=4,'z'=4,'c'=2] {'z','c'}, dimensions={0} | all-to-all | bytes 2621440 | tf_op jit(solution)/shard_map/all_to_all | solution.py:21
  119.2 9.6 %tail.1 = bf16[10240,256]{1,0:T(8,128)(2,1)} custom-call(s32[3072]{0:T(1024)} %pad.8.place_ref, bf16[2560,256]{1,0:T(8,128)(2,1)} %bitcast.24, bf16[10240,256]{1,0:T(8,128)(2,1)} %get-tuple-element.19.solved_ref, bf16[20,256,128]{2,1,0:T(8,128)(2,1)} %get-tuple-element.20.w_ref), custom_call_target="tpu_custom_call" | custom-call | flops 4000000000 | bytes 14000000 | tf_op jit(solution)/shard_map/tail/pallas_call | solution.py:342
  (14 shorter events, 0.2 us)
Async XLA Ops:
  0.6 60.8 %copy-start = (bf16[1280,640]{1,0:T(8,128)(2,1)S(1)}, bf16[1280,640]{1,0:T(8,128)(2,1)}, u32[]{:S(2)}) copy-start(bf16[1280,640]{1,0:T(8,128)(2,1)} %param.15) | copy-start | bytes 4915204
  12.5 11.5 %copy-start.2 = (f32[80,256]{1,0:T(8,128)S(1)}, f32[80,256]{1,0:T(8,128)}, u32[]{:S(2)}) copy-start(f32[80,256]{1,0:T(8,128)} %param.9) | copy-start | bytes 245764
  12.6 11.6 %copy-start.4 = (s32[256]{0:T(256)S(1)}, s32[256]{0:T(256)}, u32[]{:S(2)}) copy-start(s32[256]{0:T(256)} %param.14) | copy-start | bytes 3076
  12.6 12.6 %copy-start.3 = (s32[10,1,256]{2,1,0:T(1,128)S(1)}, s32[10,1,256]{2,1,0:T(1,128)}, u32[]{:S(2)}) copy-start(s32[10,1,256]{2,1,0:T(1,128)} %get-tuple-element.15) | copy-start | bytes 30724
  12.6 36.0 %all-to-all-start = ((bf16[128,24,256]{2,1,0:T(8,128)(2,1)}), bf16[128,24,256]{2,1,0:T(8,128)(2,1)S(1)}, u32[]{:S(2)}, u32[]{:S(2)}) async-start(bf16[128,24,256]{2,1,0:T(8,128)(2,1)} %bitcast.22), calls=%async_computation | async-start | bytes 3145728 | tf_op jit(solution)/shard_map/all_to_all | solution.py:21
  48.6 3.6 %copy-start.1 = (bf16[128,24,256]{2,1,0:T(8,128)(2,1)}, bf16[128,24,256]{2,1,0:T(8,128)(2,1)S(1)}, u32[]{:S(2)}) copy-start(bf16[128,24,256]{2,1,0:T(8,128)(2,1)S(1)} %all-to-all-done) | copy-start | bytes 4718596
  49.7 2.5 %collective-permute-start = (f32[2,80,256]{2,1,0:T(8,128)S(1)}, f32[2,80,256]{2,1,0:T(8,128)S(1)}, u32[]{:S(2)}, u32[]{:S(2)}) collective-permute-start(f32[2,80,256]{2,1,0:T(8,128)S(1)} %fusion.3), channel_id=1, source_target_pairs={{0,1},{1,0},{2,3},{3,2},{4,5},{5,4},{6,7},{7,6},{8,9},{9,8},{10,11... | collective-permute-start | bytes 491528 | tf_op jit(solution)/shard_map/ppermute | solution.py:314
  77.4 15.2 %all-to-all-start.3 = ((bf16[16,80,256]{2,1,0:T(8,128)(2,1)}), bf16[16,80,256]{2,1,0:T(8,128)(2,1)}, u32[]{:S(2)}, u32[]{:S(2)}) async-start(bf16[16,80,256]{2,1,0:T(8,128)(2,1)} %broadcast_in_dim.54), calls=%async_computation.3 | async-start | bytes 1310720 | tf_op jit(solution)/shard_map/all_to_all | solution.py:21
